TPU v7x, 512 devices: a whole 4x4x16 slice. The times are simulated.
512 devices in a mesh: clus: 32 (over y, x, core), dir: 16 (over z).
Axes of the slice: x: 4, y: 4, z: 16, core: 2. Of those that a mesh axis runs over, the one named last changes fastest.
Arguments:
- sources: bfloat16 [96, 524288], P(None, ('clus', 'dir')), may hold values from -6 to 6
- live_counts: int32 [32, 16], P('clus'), may hold values from 1 to 16, 128 in all within a row
- aggregate: bfloat16 [512, 96], replicated, may hold values from -0.625 to 0.625
- translators: bfloat16 [316, 512], P(None, 'dir'), may hold values from -0.21875 to 0.21875
- boundary_lists: int32 [32, 2, 32], P('clus'), may hold values from 0 to 255
- far_sources: int32 [8192, 128], P('clus'), may hold values from 0 to 319
- far_translators: int32 [8192, 128], P('clus'), may hold values from 0 to 315
- near_blocks: bfloat16 [8192, 96, 576], P(('clus', 'dir')), may hold values from -0.25 to 0.25
- near_columns: int32 [8192, 6], P(('clus', 'dir')), may hold values from 0 to 15
Outputs:
- field: bfloat16 [96, 524288], P(None, ('clus', 'dir'))
Inputs may be any that keep to these rules, and one draw needn't show every extreme that they name: `live_counts`: A cluster's counts add to 128; in every cluster some device holds all 16 of its slots. `far_sources`: values below 256 name the cluster's own slots, the next 32 the boxes received from the previous cluster, the last 32 those from the next cluster.
All inputs are finite; a program needn't handle non-finite values.
Results may differ from a plain program's by a relative error of at most 0.0075.
Values may be sent and summed in bfloat16 or wider, within the bound.
No kernel may reach another device: no remote copies, remote signals or barrier semaphores. Data moves between devices by JAX's collectives and lax.ppermute only.
A program may use at most 64 MiB of HBM per device.

v0:
```python
import math

import jax
import jax.numpy as jnp
from jax import lax
from jax.sharding import PartitionSpec as P

BOX_DEV = 8


def shifted(value, axis, steps):
    count = lax.axis_size(axis)
    leading, last = (max(0, -steps), min(count, count - steps))
    return lax.ppermute(value, axis, [(source, source + steps) for source in range(leading, last)])


def translate_block(block_lists, kind_table, extended):
    source_ids, kind_ids = block_lists
    kind_count = kind_table.shape[0]
    ext_slots = extended.shape[1]
    pick_kind = (
        kind_ids[:, :, None] == jnp.arange(kind_count, dtype=jnp.int32)[None, None, :]
    ).astype(jnp.bfloat16)
    values = jnp.einsum(
        "tin,nk->tik", pick_kind, kind_table, preferred_element_type=jnp.float32
    ).astype(jnp.bfloat16)
    pick_source = (
        source_ids[:, :, None] == jnp.arange(ext_slots, dtype=jnp.int32)[None, None, :]
    ).astype(jnp.bfloat16)
    weights = jnp.einsum("tis,tik->tks", pick_source, values, preferred_element_type=jnp.float32)
    weight_high = weights.astype(jnp.bfloat16)
    weight_low = (weights - weight_high.astype(jnp.float32)).astype(jnp.bfloat16)
    high_part = jnp.einsum(
        "tks,ksr->ktr", weight_high, extended, preferred_element_type=jnp.float32
    )
    low_part = jnp.einsum("tks,ksr->ktr", weight_low, extended, preferred_element_type=jnp.float32)
    return high_part + low_part


def per_device(
    sources,
    live_counts,
    aggregate,
    translators,
    boundary_lists,
    far_sources,
    far_translators,
    near_blocks,
    near_columns,
):
    dir_count = lax.axis_size("dir")
    dir_index = lax.axis_index("dir")
    unknowns = sources.shape[0]
    capacity = near_blocks.shape[0]
    rights = sources.shape[1] // capacity
    dir_slice = translators.shape[1]
    cluster_slots = far_sources.shape[0]
    interactions = far_sources.shape[1]
    neighbours = near_columns.shape[1]
    counts_here = live_counts[0]
    own_count = lax.dynamic_index_in_dim(counts_here, dir_index, 0, keepdims=False)
    own_live = jnp.arange(capacity, dtype=jnp.int32) < own_count
    local_units = (
        sources.reshape(unknowns, capacity, rights) * own_live.astype(jnp.bfloat16)[None, :, None]
    )
    masked = local_units.reshape(unknowns, capacity * rights)
    stacked = local_units[:, near_columns, :]
    blocks = near_blocks.reshape(capacity, unknowns, neighbours, unknowns)
    near_part = jnp.einsum("sujv,vsjr->usr", blocks, stacked, preferred_element_type=jnp.float32)
    gathered = lax.all_gather(masked, "dir", axis=1, tiled=True)
    upper_end = jnp.cumsum(counts_here)
    lower_end = upper_end - counts_here
    box_total = BOX_DEV * dir_count
    box_ranks = jnp.arange(box_total, dtype=jnp.int32)
    owners = jnp.sum((upper_end[None, :] <= box_ranks[:, None]).astype(jnp.int32), axis=1)
    positions = owners * capacity + box_ranks - lower_end[owners]
    direction_rows = lax.dynamic_slice_in_dim(aggregate, dir_index * dir_slice, dir_slice, 0)
    picked = gathered.reshape(unknowns, cluster_slots, rights)[:, positions, :].reshape(
        unknowns, box_total * rights
    )
    compact = jnp.dot(direction_rows, picked, preferred_element_type=jnp.float32).astype(
        jnp.bfloat16
    )
    relayed = (
        jnp.zeros((dir_slice, cluster_slots, rights), jnp.bfloat16)
        .at[:, positions, :]
        .set(compact.reshape(dir_slice, box_total, rights))
    )
    boundary_here = boundary_lists[0]
    bound_count = boundary_here.shape[1]
    upward = relayed[:, boundary_here[0], :].reshape(dir_slice, bound_count * rights)
    downward = relayed[:, boundary_here[1], :].reshape(dir_slice, bound_count * rights)
    from_before = shifted(upward, "clus", 1)
    from_after = shifted(downward, "clus", -1)
    extended = jnp.concatenate(
        [
            relayed,
            from_before.reshape(dir_slice, bound_count, rights),
            from_after.reshape(dir_slice, bound_count, rights),
        ],
        axis=1,
    )
    block_rows = math.gcd(cluster_slots, 64)
    block_count = cluster_slots // block_rows
    pieces = lax.map(
        lambda block_lists: translate_block(block_lists, translators, extended),
        (
            far_sources.reshape(block_count, block_rows, interactions),
            far_translators.reshape(block_count, block_rows, interactions),
        ),
    )
    incoming = (
        pieces.transpose(1, 0, 2, 3).reshape(dir_slice, cluster_slots * rights).astype(jnp.bfloat16)
    )
    returned = lax.all_to_all(incoming, "dir", split_axis=1, concat_axis=0, tiled=True)
    far_part = jnp.einsum("ku,kc->uc", aggregate, returned, preferred_element_type=jnp.float32)
    summed = (far_part.reshape(unknowns, capacity, rights) + near_part) * own_live.astype(
        jnp.float32
    )[None, :, None]
    return summed.reshape(unknowns, capacity * rights).astype(jnp.bfloat16)


def solution(mesh):
    in_specs = (
        P(None, ("clus", "dir")),
        P("clus", None),
        P(),
        P(None, "dir"),
        P("clus", None, None),
        P("clus", None),
        P("clus", None),
        P(("clus", "dir"), None, None),
        P(("clus", "dir"), None),
    )
    out_specs = P(None, ("clus", "dir"))
    return jax.shard_map(
        per_device, mesh=mesh, in_specs=in_specs, out_specs=out_specs, check_vma=False
    )
```

profile of v0, /device:TPU:24, one launch (start us, length us, event | category | flops | bytes accessed | tf_op | source)
XLA Modules:
  0.0 237.2 jit_solution(11071370832326165375)
XLA Ops:
  6.5 1.3 constant_dynamic-slice_fusion
  7.8 0.6 compare_convert_fusion
  8.6 1.6 broadcast_multiply_fusion.1
  10.3 0.7 copy.58
  11.2 0.7 bitcast_subtract_fusion
  11.8 0.7 fusion.34
  12.6 9.9 %fusion.27 = s32[128]{0:T(128)S(1)} fusion(s32[128]{0:T(128)S(1)} %convert_reduce_fusion, s32[]{:T(128)} %bitcast.27, s32[]{:T(128)} %bitcast.28, s32[]{:T(128)} %bitcast.29, s32[]{:T(128)} %bitcast.30, s32[]{:T(128)} %bitcast.31, s32[]{:T(128)} %bitcast.33, s32[]{:T(128)} %bitcast.32, s32[]{:T(128)} %bitcast.10, s32[]{:T(128)} %bitcast.12, s32[]{:T(128)} %bitcast.14, ...), kind=kLoop, calls=%fused_computation.65 | loop fusion | flops 4992 | bytes 1088 | tf_op jit(solution)/shard_map/select_n | solution.py:87
  22.6 0.8 fusion.28
  23.3 66.8 %all-gather.2.cloned.1.call-done = bf16[96,16384]{1,0:T(8,128)(2,1)} async-done(((bf16[96,1024]{1,0:T(8,128)(2,1)}), bf16[96,16384]{1,0:T(8,128)(2,1)}) %all-gather.2.cloned.1.call-update) | async-done | bytes 3145744 | tf_op jit(solution)/shard_map/all_gather | solution.py:70
  90.1 5.9 %copy.59 = bf16[96,16384]{0,1:T(8,128)(2,1)} copy(bf16[96,16384]{1,0:T(8,128)(2,1)} %all-gather.2.cloned.1.call-done) | data formatting | bytes 6291456 | tf_op jit(solution)/shard_map/all_gather | solution.py:70
  96.0 3.1 %gather_fusion = bf16[128,96,64]{1,2,0:T(8,128)(2,1)S(1)} fusion(bf16[96,256,64]{0,2,1:T(8,128)(2,1)} %bitcast.213, s32[1024]{0:T(1024)S(1)} %pad_clamp_fusion.3), kind=kCustom, calls=%fused_computation | custom fusion | bytes 3146240 | tf_op jit(solution)/shard_map/gather | solution.py:78
  99.1 0.9 convolution_convert_fusion
  100.0 1.1 reshape.257
  101.2 0.7 copy.60
  102.2 4.5 %scatter_fusion = bf16[32,256,64]{2,0,1:T(8,128)(2,1)S(1)} fusion(bf16[32,256,64]{2,0,1:T(8,128)(2,1)S(1)} %broadcast_in_dim.10, s32[128]{0:T(128)S(1)} %fusion.27, bf16[128,32,64]{2,1,0:T(8,128)(2,1)S(1)} %copy.60), kind=kCustom, calls=%fused_computation.4 | custom fusion | bytes 1573376 | tf_op jit(solution)/shard_map/scatter | solution.py:87
  106.6 0.6 gather_fusion.1
  107.6 1.9 collective-permute-start
  109.5 0.6 gather_fusion.2
  110.5 5.9 %collective-permute-start.1 = (bf16[32,2048]{1,0:T(8,128)(2,1)S(1)}, bf16[32,2048]{1,0:T(8,128)(2,1)S(1)}, u32[]{:S(2)}, u32[]{:S(2)}) collective-permute-start(bf16[32,2048]{1,0:T(8,128)(2,1)S(1)} %reshape.196), channel_id=1, source_target_pairs={{16,0},{32,16},{48,32},{64,48},{80,64},{96,80},{112,96},{128,112},... | collective-permute-start | bytes 393224 | tf_op jit(solution)/shard_map/ppermute | solution.py:14
  116.8 1.9 collective-permute-done.1
  119.1 2.1 pad_maximum_fusion
  121.3 4.4 %copy.65 = bf16[32,320,64]{1,2,0:T(8,128)(2,1)S(1)} copy(bf16[32,320,64]{2,0,1:T(8,128)(2,1)} %pad_maximum_fusion) | data formatting | bytes 2621440 | tf_op jit(solution)/shard_map/while | solution.py:105
  125.7 38.6 %while.10 = (s32[]{:T(128)}, bf16[4,32,64,64]{3,2,1,0:T(8,128)(2,1)}, s32[4,64,128]{2,1,0:T(8,128)}, bf16[316,32]{0,1:T(8,128)(2,1)S(1)}, s32[4,64,128]{2,1,0:T(...) while((s32[]{:T(128)}, bf16[4,32,64,64]{3,2,1,0:T(8,128)(2,1)}, s32[4,64,128]{2,1,0:T(8,128)}, ...), condition=%wide.region_4.5_spmd, body=%wide.region_3.4_spmd.sunk | while | flops 509444096 | bytes 10178897 | solution.py:105
  125.7 0.8 dynamic-slice_bitcast_fusion.3
  126.5 5.1 %subtract_convert_fusion.2 = (bf16[64,32,320]{2,1,0:T(8,128)(2,1)}, bf16[64,32,320]{2,1,0:T(8,128)(2,1)S(1)}) fusion(s32[64,128]{1,0:T(8,128)S(1)} %get-tuple-element.141, s32[64,128]{1,0:T(8,128)S(1)} %get-tuple-element.142, bf16[316,32]{0,1:T(8,128)(2,1)S(1)} %get-tuple-element.162), kind=kOutput, calls=%fused_computation.11.clone.1 | convolution fusion | flops 341540864 | bytes 2707200 | tf_op jit(solution)/shard_map/while/body/eval_jaxpr/tis,tik->tks/dot_general | solution.py:30
  131.6 2.1 fusion.54
  133.7 1.6 fusion.55
  135.4 0.8 dynamic-slice_bitcast_fusion.3
  136.2 5.1 %subtract_convert_fusion.2 = (bf16[64,32,320]{2,1,0:T(8,128)(2,1)}, bf16[64,32,320]{2,1,0:T(8,128)(2,1)S(1)}) fusion(s32[64,128]{1,0:T(8,128)S(1)} %get-tuple-element.141, s32[64,128]{1,0:T(8,128)S(1)} %get-tuple-element.142, bf16[316,32]{0,1:T(8,128)(2,1)S(1)} %get-tuple-element.162), kind=kOutput, calls=%fused_computation.11.clone.1 | convolution fusion | flops 341540864 | bytes 2707200 | tf_op jit(solution)/shard_map/while/body/eval_jaxpr/tis,tik->tks/dot_general | solution.py:30
  141.3 2.1 fusion.54
  143.4 1.6 fusion.55
  145.0 0.8 dynamic-slice_bitcast_fusion.3
  145.8 5.1 %subtract_convert_fusion.2 = (bf16[64,32,320]{2,1,0:T(8,128)(2,1)}, bf16[64,32,320]{2,1,0:T(8,128)(2,1)S(1)}) fusion(s32[64,128]{1,0:T(8,128)S(1)} %get-tuple-element.141, s32[64,128]{1,0:T(8,128)S(1)} %get-tuple-element.142, bf16[316,32]{0,1:T(8,128)(2,1)S(1)} %get-tuple-element.162), kind=kOutput, calls=%fused_computation.11.clone.1 | convolution fusion | flops 341540864 | bytes 2707200 | tf_op jit(solution)/shard_map/while/body/eval_jaxpr/tis,tik->tks/dot_general | solution.py:30
  150.9 2.1 fusion.54
  153.0 1.6 fusion.55
  154.7 0.8 dynamic-slice_bitcast_fusion.3
  155.4 5.1 %subtract_convert_fusion.2 = (bf16[64,32,320]{2,1,0:T(8,128)(2,1)}, bf16[64,32,320]{2,1,0:T(8,128)(2,1)S(1)}) fusion(s32[64,128]{1,0:T(8,128)S(1)} %get-tuple-element.141, s32[64,128]{1,0:T(8,128)S(1)} %get-tuple-element.142, bf16[316,32]{0,1:T(8,128)(2,1)S(1)} %get-tuple-element.162), kind=kOutput, calls=%fused_computation.11.clone.1 | convolution fusion | flops 341540864 | bytes 2707200 | tf_op jit(solution)/shard_map/while/body/eval_jaxpr/tis,tik->tks/dot_general | solution.py:30
  160.5 2.1 fusion.54
  162.7 1.6 fusion.55
  164.3 1.8 copy.66
  166.1 1.5 convert_element_type.55
  167.7 1.6 copy.67
  169.2 7.8 %all-to-all-start = ((bf16[32,16,1024]{2,0,1:T(8,128)(2,1)}), bf16[32,16,1024]{2,0,1:T(8,128)(2,1)S(1)}, u32[]{:S(2)}, u32[]{:S(2)}) async-start(bf16[32,16,1024]{2,0,1:T(8,128)(2,1)} %copy.67), calls=%async_computation | async-start | bytes 2097152 | tf_op jit(solution)/shard_map/all_to_all | solution.py:115
  177.4 4.2 %copy.71 = bf16[16,96,576]{1,2,0:T(8,128)(2,1)} copy(bf16[16,96,576]{2,1,0:T(8,128)(2,1)} %param.18) | data formatting | bytes 3538944 | tf_op args[7]
  181.7 0.8 gather_fusion.3
  182.6 44.1 %all-to-all-done = bf16[32,16,1024]{2,0,1:T(8,128)(2,1)S(1)} async-done(((bf16[32,16,1024]{2,0,1:T(8,128)(2,1)}), bf16[32,16,1024]{2,0,1:T(8,128)(2,1)S(1)}, u32[]{:S(2)}, u32[]{:S(2)}) %all-to-all-start) | async-done | bytes 1048608 | tf_op jit(solution)/shard_map/all_to_all | solution.py:115
  227.2 2.3 fusion.22
  229.5 0.8 copy.73
  (36 shorter events, 3.1 us)
Async XLA Ops:
  6.5 92.6 %copy-start = (bf16[512,96]{0,1:T(8,128)(2,1)S(1)}, bf16[512,96]{0,1:T(8,128)(2,1)}, u32[]{:S(2)}) copy-start(bf16[512,96]{0,1:T(8,128)(2,1)} %param.13) | copy-start | bytes 294916
  6.5 83.6 %all-gather.2.cloned.1.call-start = ((), (), s32[]{:S(2)}) async-start(), calls=%async_computation.1 | async-start | bytes 3342336 | tf_op jit(solution)/shard_map/all_gather | solution.py:70
  107.6 8.9 %collective-permute-start = (bf16[32,2048]{1,0:T(8,128)(2,1)S(1)}, bf16[32,2048]{1,0:T(8,128)(2,1)S(1)}, u32[]{:S(2)}, u32[]{:S(2)}) collective-permute-start(bf16[32,2048]{1,0:T(8,128)(2,1)S(1)} %reshape.194), channel_id=1, source_target_pairs={{0,16},{16,32},{32,48},{48,64},{64,80},{80,96},{96,112},{112,128},... | collective-permute-start | bytes 393224 | tf_op jit(solution)/shard_map/ppermute | solution.py:14
  110.5 8.3 %collective-permute-start.1 = (bf16[32,2048]{1,0:T(8,128)(2,1)S(1)}, bf16[32,2048]{1,0:T(8,128)(2,1)S(1)}, u32[]{:S(2)}, u32[]{:S(2)}) collective-permute-start(bf16[32,2048]{1,0:T(8,128)(2,1)S(1)} %reshape.196), channel_id=1, source_target_pairs={{16,0},{32,16},{48,32},{64,48},{80,64},{96,80},{112,96},{128,112},... | collective-permute-start | bytes 393224 | tf_op jit(solution)/shard_map/ppermute | solution.py:14
  121.3 4.5 %copy-start.3 = (bf16[316,32]{0,1:T(8,128)(2,1)S(1)}, bf16[316,32]{0,1:T(8,128)(2,1)}, u32[]{:S(2)}) copy-start(bf16[316,32]{0,1:T(8,128)(2,1)} %param.14) | copy-start | bytes 60676
  167.6 9.4 %copy-start.1 = (bf16[96,1024]{1,0:T(8,128)(2,1)S(1)}, bf16[96,1024]{1,0:T(8,128)(2,1)}, u32[]{:S(2)}) copy-start(bf16[96,1024]{1,0:T(8,128)(2,1)} %param.11) | copy-start | bytes 589828
  167.7 9.6 %copy-start.2 = (s32[16,6]{0,1:T(8,128)S(1)}, s32[16,6]{0,1:T(8,128)}, u32[]{:S(2)}) copy-start(s32[16,6]{0,1:T(8,128)} %param.19) | copy-start | bytes 1156
  169.2 57.5 %all-to-all-start = ((bf16[32,16,1024]{2,0,1:T(8,128)(2,1)}), bf16[32,16,1024]{2,0,1:T(8,128)(2,1)S(1)}, u32[]{:S(2)}, u32[]{:S(2)}) async-start(bf16[32,16,1024]{2,0,1:T(8,128)(2,1)} %copy.67), calls=%async_computation | async-start | bytes 2097152 | tf_op jit(solution)/shard_map/all_to_all | solution.py:115
Sparse Core Ops, SparseCore 0:
  10.4 79.6 all-gather.1
where the time goes:
time: 239 us; the launch traced here: 237 us
  waiting for transfers between devices  113 us (47%)
  local copies, waits for them, and re-layouts  39.9 us (17%)
  matrix products  38.9 us (16%)
  other arithmetic  16.1 us (7%)
  starting transfers between devices  15.6 us (7%)
  between operations  13.7 us (6%)
    all_gather x1, waiting for transfers between devices, per_device(): gathered = lax.all_gather(masked, 'dir', axis=1, tiled=True)  66.8 us
    all_to_all x1, waiting for transfers between devices, per_device(): lax.all_to_all(incoming, 'dir', split_axis=1, concat_axis=0, tiled=True)  44.1 us
    dot_general x4, matrix products, translate_block(): jnp.einsum('tis,tik->tks', pick_source, values, preferred_element_type=jn...  20.4 us
    select_n x1, other arithmetic, per_device(): relayed = jnp.zeros((dir_slice, cluster_slots, rights), jnp.bfloat16).at[...  9.93 us
    dot_general x4, matrix products, translate_block(): jnp.einsum('tks,ksr->ktr', weight_low, extended, preferred_element_type=j...  8.55 us
    ppermute x2, starting transfers between devices, shifted(): lax.ppermute(value, axis, [(source, source + steps) for source in range(l...  7.85 us
    all_to_all x1, starting transfers between devices, per_device(): lax.all_to_all(incoming, 'dir', split_axis=1, concat_axis=0, tiled=True)  7.79 us
    dot_general x4, matrix products, translate_block(): jnp.einsum('tks,ksr->ktr', weight_high, extended, preferred_element_type=...  6.52 us
  transfers between devices with their start and end apart: 4, of which 3 were waited for; matrix products, arithmetic and copies ran while one was open for 8% of the time, Pallas kernels for 0%

commit v1 on v0

v1 whole, which is shorter than its diff:
```python
import jax
import jax.numpy as jnp
from jax import lax
from jax.experimental import pallas as pl
from jax.experimental.pallas import tpu as pltpu
from jax.sharding import PartitionSpec as P

U = 96
K = 512
R = 64
NTR = 316
NI = 128
NN = 6
NBND = 32
BCAP = 16
S_CL = 256
S_EXT = 320
N_DIR = 16
RD = R // N_DIR
KC = K // 128
NTR_PAD = 320
F32 = jnp.float32
BF16 = jnp.bfloat16


def shifted(value, axis, steps):
    count = lax.axis_size(axis)
    leading, last = (max(0, -steps), min(count, count - steps))
    return lax.ppermute(value, axis, [(source, source + steps) for source in range(leading, last)])


def deal_kernel(src_ref, out_ref, rows):
    for pair in range(BCAP // 2):
        turned = src_ref[:, pair * 128 : (pair + 1) * 128].astype(F32).T
        for half in range(2):
            rows[pl.ds(2 * pair + half, R, stride=BCAP), :] = turned[half * R : (half + 1) * R]
    out_ref[...] = rows[...].reshape(N_DIR, RD, BCAP, U).astype(BF16)


def boundary_kernel(recv_ref, list_ref, live_ref, up_ref, down_ref):
    slots = lax.broadcasted_iota(jnp.int32, (2 * NBND, S_CL), 1)
    pick = ((slots == list_ref[...]) & (live_ref[...] > 0)).astype(F32).astype(BF16)
    for r in range(RD):
        units = recv_ref[:, r].reshape(S_CL, U)
        chosen = jnp.dot(pick, units, preferred_element_type=F32).astype(BF16)
        up_ref[r] = chosen[:NBND]
        down_ref[r] = chosen[NBND:]


def far_kernel(
    pairs, counts, recv_ref, live_ref, before_ref, after_ref, kinds_ref, agg_ref, out_ref, ext, table, incoming
):
    agg = agg_ref[...]
    for r in range(RD):
        own = jnp.dot(recv_ref[:, r].reshape(S_CL, U), agg, preferred_element_type=F32)
        own = jnp.where(live_ref[...] > 0, own, 0.0)
        prev = jnp.dot(before_ref[r], agg, preferred_element_type=F32)
        foll = jnp.dot(after_ref[r], agg, preferred_element_type=F32)
        for c in range(KC):
            lanes = slice(c * 128, (c + 1) * 128)
            at = r * KC + c
            ext[pl.ds(at, S_CL, stride=16), :] = own[:, lanes]
            ext[pl.ds(S_CL * 16 + at, NBND, stride=16), :] = prev[:, lanes]
            ext[pl.ds((S_CL + NBND) * 16 + at, NBND, stride=16), :] = foll[:, lanes]
    eye = lax.broadcasted_iota(jnp.int32, (NTR_PAD, NTR), 0) == lax.broadcasted_iota(
        jnp.int32, (NTR_PAD, NTR), 1
    )
    kinds = lax.dot_general(
        eye.astype(F32).astype(BF16),
        kinds_ref[...],
        (((1,), (1,)), ((), ())),
        preferred_element_type=F32,
    )
    for c in range(KC):
        part = kinds[:, c * 128 : (c + 1) * 128]
        table[pl.ds(c, NTR_PAD, stride=8), :] = part
        table[pl.ds(c + KC, NTR_PAD, stride=8), :] = part
    incoming[...] = jnp.zeros_like(incoming)

    def device(d, carry):
        def target(j, inner):
            t = d * BCAP + j
            sums = [[jnp.zeros((8, 128), F32) for _ in range(2)] for _ in range(2)]
            for i in range(NI):
                word = pairs[t, i]
                n8 = pl.multiple_of(word & 0xFFFF, 8)
                s16 = pl.multiple_of(lax.shift_right_logical(word, 16), 16)
                weight = table[pl.ds(n8, 8), :]
                for h in range(2):
                    sums[i % 2][h] = sums[i % 2][h] + weight * ext[pl.ds(s16 + 8 * h, 8), :]
            for h in range(2):
                incoming[pl.ds(pl.multiple_of(t * 16 + 8 * h, 8), 8), :] = sums[0][h] + sums[1][h]
            return inner

        return lax.fori_loop(0, counts[d], target, carry)

    lax.fori_loop(0, N_DIR, device, 0)
    for r in range(RD):
        far = jnp.zeros((S_CL, U), F32)
        for c in range(KC):
            part = incoming[pl.ds(r * KC + c, S_CL, stride=16), :].astype(BF16)
            far = far + lax.dot_general(
                part,
                agg[:, c * 128 : (c + 1) * 128],
                (((1,), (1,)), ((), ())),
                preferred_element_type=F32,
            )
        out_ref[:, r] = far.reshape(N_DIR, BCAP, U).astype(BF16)


def near_kernel(columns, count, src_ref, blocks_ref, out_ref, units, stack):
    for pair in range(BCAP // 2):
        both = src_ref[:, pair * 128 : (pair + 1) * 128].astype(F32)
        for half in range(2):
            slot = 2 * pair + half
            own = both[:, half * R : (half + 1) * R]
            units[slot] = jnp.where(count[0] > slot, own, 0.0).astype(BF16)
    for pair in range(BCAP // 2):
        halves = []
        for half in range(2):
            slot = 2 * pair + half
            for j in range(NN):
                stack[j * U : (j + 1) * U, :] = units[columns[slot, j]]
            halves.append(jnp.dot(blocks_ref[slot], stack[...], preferred_element_type=F32))
        out_ref[:, pair * 128 : (pair + 1) * 128] = jnp.concatenate(halves, axis=1)


def finish_kernel(count, back_ref, near_ref, out_ref, rows):
    rows[...] = back_ref[...].astype(F32).reshape(R * BCAP, U)
    for pair in range(BCAP // 2):
        halves = [rows[pl.ds(2 * pair + half, R, stride=BCAP), :] for half in range(2)]
        far = jnp.concatenate(halves, axis=0).T
        cols = slice(pair * 128, (pair + 1) * 128)
        slot = 2 * pair + lax.broadcasted_iota(jnp.int32, (U, 128), 1) // R
        out_ref[:, cols] = jnp.where(slot < count[0], far + near_ref[:, cols], 0.0).astype(BF16)


VM = pl.BlockSpec(memory_space=pltpu.VMEM)
SM = pl.BlockSpec(memory_space=pltpu.SMEM)


def per_device(
    sources,
    live_counts,
    aggregate,
    translators,
    boundary_lists,
    far_sources,
    far_translators,
    near_blocks,
    near_columns,
):
    dir_index = lax.axis_index("dir")
    counts = live_counts[0]
    own_count = lax.dynamic_slice(counts, (dir_index,), (1,))
    slot_ids = jnp.arange(S_CL, dtype=jnp.int32)
    live = (slot_ids % BCAP < jnp.repeat(counts, BCAP)).astype(jnp.int32)

    send = pl.pallas_call(
        deal_kernel,
        out_shape=jax.ShapeDtypeStruct((N_DIR, RD, BCAP, U), BF16),
        in_specs=[VM],
        out_specs=VM,
        scratch_shapes=[pltpu.VMEM((R * BCAP, U), F32)],
        name="deal",
    )(sources)
    recv = lax.all_to_all(send, "dir", split_axis=0, concat_axis=0, tiled=True)
    kinds = lax.all_to_all(
        jnp.broadcast_to(translators.T[None], (N_DIR, K // N_DIR, NTR)),
        "dir",
        split_axis=0,
        concat_axis=0,
        tiled=True,
    ).reshape(K, NTR)

    up, down = pl.pallas_call(
        boundary_kernel,
        out_shape=[jax.ShapeDtypeStruct((RD, NBND, U), BF16)] * 2,
        in_specs=[VM, VM, VM],
        out_specs=[VM, VM],
        name="boundary",
    )(recv, boundary_lists.reshape(2 * NBND, 1), live.reshape(1, S_CL))
    before = shifted(up, "clus", 1)
    after = shifted(down, "clus", -1)

    near = pl.pallas_call(
        near_kernel,
        out_shape=jax.ShapeDtypeStruct((U, BCAP * R), F32),
        in_specs=[SM, SM, VM, VM],
        out_specs=VM,
        scratch_shapes=[pltpu.VMEM((BCAP, U, R), BF16), pltpu.VMEM((NN * U, R), BF16)],
        name="near",
    )(near_columns, own_count, sources, near_blocks)

    pairs = far_sources * (16 << 16) + far_translators * 8
    far = pl.pallas_call(
        far_kernel,
        out_shape=jax.ShapeDtypeStruct((N_DIR, RD, BCAP, U), BF16),
        in_specs=[SM, SM, VM, VM, VM, VM, VM, VM],
        out_specs=VM,
        scratch_shapes=[
            pltpu.VMEM((S_EXT * 16, 128), F32),
            pltpu.VMEM((NTR_PAD * 8, 128), F32),
            pltpu.VMEM((S_CL * 16, 128), F32),
        ],
        name="far",
    )(pairs, counts, recv, live.reshape(S_CL, 1), before, after, kinds, aggregate.T)
    back = lax.all_to_all(far, "dir", split_axis=0, concat_axis=0, tiled=True)

    return pl.pallas_call(
        finish_kernel,
        out_shape=jax.ShapeDtypeStruct((U, BCAP * R), BF16),
        in_specs=[SM, VM, VM],
        out_specs=VM,
        scratch_shapes=[pltpu.VMEM((R * BCAP, U), F32)],
        name="finish",
    )(own_count, back, near)


def solution(mesh):
    in_specs = (
        P(None, ("clus", "dir")),
        P("clus", None),
        P(),
        P(None, "dir"),
        P("clus", None, None),
        P("clus", None),
        P("clus", None),
        P(("clus", "dir"), None, None),
        P(("clus", "dir"), None),
    )
    out_specs = P(None, ("clus", "dir"))
    return jax.shard_map(
        per_device, mesh=mesh, in_specs=in_specs, out_specs=out_specs, check_vma=False
    )
```

time: 239 us -> 134 us (0.56)
  waiting for transfers between devices: 113 us -> 23.8 us
  Pallas kernels: 0 us -> 48.8 us
  matrix products: 38.9 us -> 0 us
  local copies, waits for them, and re-layouts: 39.9 us -> 5.46 us
  blocking collectives: 0 us -> 33.7 us
  other arithmetic: 16.1 us -> 1.95 us
  between operations: 13.7 us -> 0.09 us
  starting transfers between devices: 15.6 us -> 19.5 us
    all_gather x1 -> x0, waiting for transfers between devices: 66.8 us -> none  [per_device(): gathered = lax.all_gather(masked, 'dir', axis=1, tiled=True)]
    pallas_call x0 -> x5, Pallas kernels: none -> 48.8 us  [the longest x1 38.2 us: per_device(): pl.pallas_call(far_kernel, out_shape=jax.ShapeDtypeStruct((N_DIR, RD, BCA...]
    dot_general x15 -> x0, matrix products: 38.9 us -> none  [the longest x4 20.4 us: translate_block(): jnp.einsum('tis,tik->tks', pick_source, values, preferred_element_type=jn...]
    all_to_all x0 -> x1, blocking collectives: none -> 33.7 us  [per_device(): recv = lax.all_to_all(send, 'dir', split_axis=0, concat_axis=0, tiled=True)]
    all_to_all x1 -> x2, waiting for transfers between devices: 44.1 us -> 22.8 us  [the longest x1 12.7 us: per_device(): back = lax.all_to_all(far, 'dir', split_axis=0, concat_axis=0, tiled=True)]
    select_n x3 -> x0, other arithmetic: 10.7 us -> none  [the longest x1 9.93 us: per_device(): relayed = jnp.zeros((dir_slice, cluster_slots, rights), jnp.bfloat16).at[...]
    gather x7 -> x0, local copies, waits for them, and re-layouts: 6.11 us -> none  [the longest x1 3.14 us: per_device(): gathered.reshape(unknowns, cluster_slots, rights)[:, positions, :]]
    all_gather x1 -> x0, local copies, waits for them, and re-layouts: 5.86 us -> none  [per_device(): gathered = lax.all_gather(masked, 'dir', axis=1, tiled=True)]
  transfers between devices with their start and end apart: 4 -> 4, of which waited for: 3 -> 3; matrix products, arithmetic and copies ran while one was open for 8% -> 3% of each run, Pallas kernels for 0% -> 5%
where the time goes in v1:
time: 134 us; the launch traced here: 133 us
  Pallas kernels  48.8 us (36%)
  blocking collectives  33.7 us (25%)
  waiting for transfers between devices  23.8 us (18%)
  starting transfers between devices  19.5 us (15%)
  local copies, waits for them, and re-layouts  5.46 us (4%)
  other arithmetic  1.95 us (1%)
    pallas_call x1, Pallas kernels, per_device(): pl.pallas_call(far_kernel, out_shape=jax.ShapeDtypeStruct((N_DIR, RD, BCA...  38.2 us
    all_to_all x1, blocking collectives, per_device(): recv = lax.all_to_all(send, 'dir', split_axis=0, concat_axis=0, tiled=True)  33.7 us
    all_to_all x1, waiting for transfers between devices, per_device(): back = lax.all_to_all(far, 'dir', split_axis=0, concat_axis=0, tiled=True)  12.7 us
    all_to_all x1, waiting for transfers between devices, per_device(): lax.all_to_all(jnp.broadcast_to(translators.T[None], (N_DIR, K // N_DIR,...  10 us
    ppermute x2, starting transfers between devices, shifted(): lax.ppermute(value, axis, [(source, source + steps) for source in range(l...  7.66 us
    all_to_all x1, starting transfers between devices, per_device(): back = lax.all_to_all(far, 'dir', split_axis=0, concat_axis=0, tiled=True)  6.02 us
    all_to_all x1, starting transfers between devices, per_device(): lax.all_to_all(jnp.broadcast_to(translators.T[None], (N_DIR, K // N_DIR,...  5.77 us
    pallas_call x1, Pallas kernels, per_device(): pl.pallas_call(near_kernel, out_shape=jax.ShapeDtypeStruct((U, BCAP * R),...  4.25 us
  transfers between devices with their start and end apart: 4, of which 3 were waited for; matrix products, arithmetic and copies ran while one was open for 3% of the time, Pallas kernels for 5%

profile of v1, /device:TPU:24, one launch (start us, length us, event | category | flops | bytes accessed | tf_op | source)
XLA Modules:
  0.0 133.2 jit_solution(6072797421105087748)
XLA Ops:
  0.0 0.0 copy-start.7
  0.0 0.0 copy-start.9
  0.0 0.0 copy-start.3
  0.0 0.0 copy-start.2
  0.0 1.9 %deal.1 = bf16[16,4,16,96]{3,2,1,0:T(8,128)(2,1)} custom-call(bf16[96,1024]{1,0:T(8,128)(2,1)} %src_ref.3), custom_call_target="tpu_custom_call" | custom-call | tf_op jit(solution)/shard_map/deal/pallas_call | solution.py:159
  1.9 33.7 %all_to_all.15.recv_ref = bf16[16,4,16,96]{3,2,1,0:T(8,128)(2,1)} all-to-all(bf16[16,4,16,96]{3,2,1,0:T(8,128)(2,1)} %deal.1), channel_id=1, replica_groups=mesh['clus'=32,'dir'=16] {'dir'}, dimensions={0} | all-to-all | bytes 393216 | tf_op jit(solution)/shard_map/all_to_all | solution.py:167
  35.6 0.0 copy-start.8
  35.6 0.0 copy-start.6
  35.6 1.6 %broadcast_in_dim.10 = bf16[16,32,316]{2,1,0:T(8,128)(2,1)} broadcast(bf16[32,316]{1,0:T(8,128)(2,1)} %bitcast.7), dimensions={1,2} | broadcast | bytes 343808 | tf_op jit(solution)/shard_map/broadcast_in_dim | solution.py:169
  37.2 5.8 %all-to-all-start.1 = ((bf16[16,32,316]{2,1,0:T(8,128)(2,1)}), bf16[16,32,316]{2,1,0:T(8,128)(2,1)S(1)}, u32[]{:S(2)}, u32[]{:S(2)}) async-start(bf16[16,32,316]{2,1,0:T(8,128)(2,1)} %broadcast_in_dim.10), calls=%async_computation.1 | async-start | bytes 786432 | tf_op jit(solution)/shard_map/all_to_all | solution.py:168
  43.0 0.0 copy-done.7
  43.0 0.1 broadcast_in_dim.4
  43.0 0.1 reshape.87
  43.1 0.1 reshape.85
  43.2 0.0 copy-done.9
  43.2 0.7 reshape.89.list_ref
  43.9 0.6 compare_convert_fusion.live_ref
  44.5 0.0 copy-done.3
  44.5 0.0 copy-done.2
  44.5 0.7 multiply_add_fusion.pairs
  45.2 1.8 %boundary.1 = (bf16[4,32,96]{2,1,0:T(8,128)(2,1)}, bf16[4,32,96]{2,1,0:T(8,128)(2,1)}) custom-call(bf16[16,4,16,96]{3,2,1,0:T(8,128)(2,1)} %all_to_all.15.recv_ref, s32[64,1]{1,0:T(8,128)} %reshape.89.list_ref, s32[1,256]{1,0:T(1,128)} %compare_convert_fusion.live_ref), custom_call_target="tpu_custom_call" | custom-call | tf_op jit(solution)/shard_map/boundary/pallas_call | solution.py:176
  47.0 1.9 %collective-permute-start = (bf16[4,32,96]{2,1,0:T(8,128)(2,1)}, bf16[4,32,96]{2,1,0:T(8,128)(2,1)S(1)}, u32[]{:S(2)}, u32[]{:S(2)}) collective-permute-start(bf16[4,32,96]{2,1,0:T(8,128)(2,1)} %get-tuple-element.7), channel_id=1, source_target_pairs={{0,16},{16,32},{32,48},{48,64},{64,80},{80,96},{96,112},{112,128},... | collective-permute-start | bytes 73736 | tf_op jit(solution)/shard_map/ppermute | solution.py:29
  49.0 5.8 %collective-permute-start.1 = (bf16[4,32,96]{2,1,0:T(8,128)(2,1)}, bf16[4,32,96]{2,1,0:T(8,128)(2,1)S(1)}, u32[]{:S(2)}, u32[]{:S(2)}) collective-permute-start(bf16[4,32,96]{2,1,0:T(8,128)(2,1)} %get-tuple-element.8), channel_id=1, source_target_pairs={{16,0},{32,16},{48,32},{64,48},{80,64},{96,80},{112,96},{128,112},... | collective-permute-start | bytes 73736 | tf_op jit(solution)/shard_map/ppermute | solution.py:29
  54.7 0.2 copy.15
  54.9 0.7 convert_element_type.19.live_ref
  55.6 0.0 collective-permute-done.before_ref
  55.6 0.0 copy-start.4
  55.6 1.0 collective-permute-done.1.after_ref
  56.6 0.0 copy-start.5
  56.6 10.0 %all-to-all-done.1 = bf16[16,32,316]{2,1,0:T(8,128)(2,1)S(1)} async-done(((bf16[16,32,316]{2,1,0:T(8,128)(2,1)}), bf16[16,32,316]{2,1,0:T(8,128)(2,1)S(1)}, u32[]{:S(2)}, u32[]{:S(2)}) %all-to-all-start.1) | async-done | bytes 323616 | tf_op jit(solution)/shard_map/all_to_all | solution.py:168
  66.6 0.0 copy-start
  66.6 0.0 copy-done.4
  66.6 0.0 copy-done.5
  66.6 0.8 copy-done
  67.4 38.2 %far.1 = bf16[16,4,16,96]{3,2,1,0:T(8,128)(2,1)} custom-call(s32[256,128]{1,0:T(8,128)} %multiply_add_fusion.pairs, s32[16]{0:T(128)} %bitcast.8, bf16[16,4,16,96]{3,2,1,0:T(8,128)(2,1)} %all_to_all.15.recv_ref, s32[256,1]{1,0:T(8,128)} %convert_element_type.19.live_ref, bf16[4,32,96]{2,1,0:T(8,128)(2,1)} %copy-done.4, bf16[4,32,96]{2,1,0:T(8,128)(2,1)} %copy-done.5, ...), custom_call_target="tpu_custom_call" | custom-call | tf_op jit(solution)/shard_map/far/pallas_call | solution.py:196
  105.5 6.0 %all-to-all-start.2 = ((bf16[16,4,16,96]{3,2,1,0:T(8,128)(2,1)}), bf16[16,4,16,96]{3,2,1,0:T(8,128)(2,1)S(1)}, u32[]{:S(2)}, u32[]{:S(2)}) async-start(bf16[16,4,16,96]{3,2,1,0:T(8,128)(2,1)} %far.1), calls=%async_computation.2 | async-start | bytes 524288 | tf_op jit(solution)/shard_map/all_to_all | solution.py:208
  111.6 0.0 copy-done.8
  111.6 0.6 constant_dynamic-slice_fusion
  112.2 0.0 copy-done.6
  112.2 0.7 copy.17.columns
  112.9 4.3 %near.1.near_ref = f32[96,1024]{1,0:T(8,128)} custom-call(s32[16,6]{1,0:T(8,128)} %copy.17.columns, s32[1]{0:T(128)} %bitcast.count, bf16[96,1024]{1,0:T(8,128)(2,1)} %src_ref.3, bf16[16,96,576]{2,1,0:T(8,128)(2,1)} %blocks_ref.1), custom_call_target="tpu_custom_call" | custom-call | tf_op jit(solution)/shard_map/near/pallas_call | solution.py:186
  117.1 12.7 %all-to-all-done.2.back_ref = bf16[16,4,16,96]{3,2,1,0:T(8,128)(2,1)S(1)} async-done(((bf16[16,4,16,96]{3,2,1,0:T(8,128)(2,1)}), bf16[16,4,16,96]{3,2,1,0:T(8,128)(2,1)S(1)}, u32[]{:S(2)}, u32[]{:S(2)}) %all-to-all-start.2) | async-done | bytes 196640 | tf_op jit(solution)/shard_map/all_to_all | solution.py:208
  129.9 0.0 copy-start.1
  129.9 0.7 copy-done.1
  130.6 2.6 %finish.1 = bf16[96,1024]{1,0:T(8,128)(2,1)} custom-call(s32[1]{0:T(128)} %bitcast.count, bf16[16,4,16,96]{3,2,1,0:T(8,128)(2,1)} %copy-done.1, f32[96,1024]{1,0:T(8,128)} %near.1.near_ref), custom_call_target="tpu_custom_call" | custom-call | tf_op jit(solution)/shard_map/finish/pallas_call | solution.py:210
  (1 shorter events, 0.0 us)
Async XLA Ops:
  0.0 43.0 %copy-start.7 = (s32[1,16]{1,0:T(1,128)S(1)}, s32[1,16]{1,0:T(1,128)}, u32[]{:S(2)}) copy-start(s32[1,16]{1,0:T(1,128)} %param.10) | copy-start | bytes 196
  0.0 43.2 %copy-start.9 = (s32[1,2,32]{2,1,0:T(2,128)S(1)}, s32[1,2,32]{2,1,0:T(2,128)}, u32[]{:S(2)}) copy-start(s32[1,2,32]{2,1,0:T(2,128)} %param.13) | copy-start | bytes 772
  0.0 44.5 %copy-start.3 = (s32[256,128]{1,0:T(8,128)S(1)}, s32[256,128]{1,0:T(8,128)}, u32[]{:S(2)}) copy-start(s32[256,128]{1,0:T(8,128)} %param.14) | copy-start | bytes 393220
  0.0 44.5 %copy-start.2 = (s32[256,128]{1,0:T(8,128)S(1)}, s32[256,128]{1,0:T(8,128)}, u32[]{:S(2)}) copy-start(s32[256,128]{1,0:T(8,128)} %param.15) | copy-start | bytes 393220
  35.6 76.0 %copy-start.8 = (s32[1,16]{1,0:T(1,128)S(1)}, s32[1,16]{1,0:T(1,128)}, u32[]{:S(2)}) copy-start(s32[1,16]{1,0:T(1,128)} %param.10) | copy-start | bytes 196
  35.6 76.6 %copy-start.6 = (s32[16,6]{0,1:T(8,128)S(1)}, s32[16,6]{0,1:T(8,128)}, u32[]{:S(2)}) copy-start(s32[16,6]{0,1:T(8,128)} %param.17) | copy-start | bytes 1156
  37.2 29.5 %all-to-all-start.1 = ((bf16[16,32,316]{2,1,0:T(8,128)(2,1)}), bf16[16,32,316]{2,1,0:T(8,128)(2,1)S(1)}, u32[]{:S(2)}, u32[]{:S(2)}) async-start(bf16[16,32,316]{2,1,0:T(8,128)(2,1)} %broadcast_in_dim.10), calls=%async_computation.1 | async-start | bytes 786432 | tf_op jit(solution)/shard_map/all_to_all | solution.py:168
  47.0 8.6 %collective-permute-start = (bf16[4,32,96]{2,1,0:T(8,128)(2,1)}, bf16[4,32,96]{2,1,0:T(8,128)(2,1)S(1)}, u32[]{:S(2)}, u32[]{:S(2)}) collective-permute-start(bf16[4,32,96]{2,1,0:T(8,128)(2,1)} %get-tuple-element.7), channel_id=1, source_target_pairs={{0,16},{16,32},{32,48},{48,64},{64,80},{80,96},{96,112},{112,128},... | collective-permute-start | bytes 73736 | tf_op jit(solution)/shard_map/ppermute | solution.py:29
  49.0 7.7 %collective-permute-start.1 = (bf16[4,32,96]{2,1,0:T(8,128)(2,1)}, bf16[4,32,96]{2,1,0:T(8,128)(2,1)S(1)}, u32[]{:S(2)}, u32[]{:S(2)}) collective-permute-start(bf16[4,32,96]{2,1,0:T(8,128)(2,1)} %get-tuple-element.8), channel_id=1, source_target_pairs={{16,0},{32,16},{48,32},{64,48},{80,64},{96,80},{112,96},{128,112},... | collective-permute-start | bytes 73736 | tf_op jit(solution)/shard_map/ppermute | solution.py:29
  55.6 11.1 %copy-start.4 = (bf16[4,32,96]{2,1,0:T(8,128)(2,1)}, bf16[4,32,96]{2,1,0:T(8,128)(2,1)S(1)}, u32[]{:S(2)}) copy-start(bf16[4,32,96]{2,1,0:T(8,128)(2,1)S(1)} %collective-permute-done.before_ref) | copy-start | bytes 73732
  56.6 10.0 %copy-start.5 = (bf16[4,32,96]{2,1,0:T(8,128)(2,1)}, bf16[4,32,96]{2,1,0:T(8,128)(2,1)S(1)}, u32[]{:S(2)}) copy-start(bf16[4,32,96]{2,1,0:T(8,128)(2,1)S(1)} %collective-permute-done.1.after_ref) | copy-start | bytes 73732
  66.6 0.8 copy-start
  105.5 24.3 %all-to-all-start.2 = ((bf16[16,4,16,96]{3,2,1,0:T(8,128)(2,1)}), bf16[16,4,16,96]{3,2,1,0:T(8,128)(2,1)S(1)}, u32[]{:S(2)}, u32[]{:S(2)}) async-start(bf16[16,4,16,96]{3,2,1,0:T(8,128)(2,1)} %far.1), calls=%async_computation.2 | async-start | bytes 524288 | tf_op jit(solution)/shard_map/all_to_all | solution.py:208
  129.9 0.7 copy-start.1

commit v2 on v1

--- a/solution.py
+++ b/solution.py
@@ -16,9 +16,11 @@
 S_CL = 256
 S_EXT = 320
 N_DIR = 16
+KD = K // N_DIR
 RD = R // N_DIR
 KC = K // 128
 NTR_PAD = 320
+LAST = (S_CL - 1) * NI + 1
 F32 = jnp.float32
 BF16 = jnp.bfloat16
 
@@ -29,30 +31,54 @@
     return lax.ppermute(value, axis, [(source, source + steps) for source in range(leading, last)])
 
 
-def deal_kernel(src_ref, out_ref, rows):
-    for pair in range(BCAP // 2):
-        turned = src_ref[:, pair * 128 : (pair + 1) * 128].astype(F32).T
+def deal_kernel(src_ref, kinds_ref, out_ref, rows, wide):
+    for pair in range(BCAP // 2):
+        both = src_ref[:, pair * 128 : (pair + 1) * 128].astype(F32)
+        both = jnp.concatenate([both, jnp.zeros((128 - U, 128), F32)], axis=0).T
         for half in range(2):
-            rows[pl.ds(2 * pair + half, R, stride=BCAP), :] = turned[half * R : (half + 1) * R]
-    out_ref[...] = rows[...].reshape(N_DIR, RD, BCAP, U).astype(BF16)
+            rows[pl.ds(2 * pair + half, R, stride=BCAP), :] = both[half * R : (half + 1) * R]
+    wide[...] = jnp.zeros_like(wide)
+    wide[:, :NTR] = kinds_ref[...].astype(F32)
+    last = wide[:, 256:384]
+    spare = jnp.concatenate([pltpu.roll(last, U, 1), pltpu.roll(last, U - KD, 1)], axis=0)
+    in_spare = lax.broadcasted_iota(jnp.int32, (RD * BCAP, 128), 1) >= U
+    tail = jnp.concatenate([wide[:, :128], wide[:, 128:256]], axis=0).astype(BF16)
+    for d in range(N_DIR):
+        block = rows[d * RD * BCAP : (d + 1) * RD * BCAP, :]
+        out_ref[d, : RD * BCAP] = jnp.where(in_spare, spare, block).astype(BF16)
+        out_ref[d, RD * BCAP :] = tail
+
+
+def units_of(recv_ref, r):
+    return recv_ref[:, r * BCAP : (r + 1) * BCAP].reshape(S_CL, 128)
 
 
 def boundary_kernel(recv_ref, list_ref, live_ref, up_ref, down_ref):
     slots = lax.broadcasted_iota(jnp.int32, (2 * NBND, S_CL), 1)
     pick = ((slots == list_ref[...]) & (live_ref[...] > 0)).astype(F32).astype(BF16)
     for r in range(RD):
-        units = recv_ref[:, r].reshape(S_CL, U)
-        chosen = jnp.dot(pick, units, preferred_element_type=F32).astype(BF16)
+        chosen = jnp.dot(pick, units_of(recv_ref, r), preferred_element_type=F32).astype(BF16)
         up_ref[r] = chosen[:NBND]
         down_ref[r] = chosen[NBND:]
 
 
 def far_kernel(
-    pairs, counts, recv_ref, live_ref, before_ref, after_ref, kinds_ref, agg_ref, out_ref, ext, table, incoming
+    kind_rows,
+    source_rows,
+    counts,
+    recv_ref,
+    live_ref,
+    before_ref,
+    after_ref,
+    agg_ref,
+    out_ref,
+    ext,
+    table,
+    incoming,
 ):
     agg = agg_ref[...]
     for r in range(RD):
-        own = jnp.dot(recv_ref[:, r].reshape(S_CL, U), agg, preferred_element_type=F32)
+        own = jnp.dot(units_of(recv_ref, r), agg, preferred_element_type=F32)
         own = jnp.where(live_ref[...] > 0, own, 0.0)
         prev = jnp.dot(before_ref[r], agg, preferred_element_type=F32)
         foll = jnp.dot(after_ref[r], agg, preferred_element_type=F32)
@@ -62,29 +88,30 @@
             ext[pl.ds(at, S_CL, stride=16), :] = own[:, lanes]
             ext[pl.ds(S_CL * 16 + at, NBND, stride=16), :] = prev[:, lanes]
             ext[pl.ds((S_CL + NBND) * 16 + at, NBND, stride=16), :] = foll[:, lanes]
-    eye = lax.broadcasted_iota(jnp.int32, (NTR_PAD, NTR), 0) == lax.broadcasted_iota(
-        jnp.int32, (NTR_PAD, NTR), 1
-    )
-    kinds = lax.dot_general(
-        eye.astype(F32).astype(BF16),
-        kinds_ref[...],
-        (((1,), (1,)), ((), ())),
-        preferred_element_type=F32,
-    )
-    for c in range(KC):
-        part = kinds[:, c * 128 : (c + 1) * 128]
-        table[pl.ds(c, NTR_PAD, stride=8), :] = part
-        table[pl.ds(c + KC, NTR_PAD, stride=8), :] = part
+    for first, count, lane, row in ((0, 128, 0, 64), (128, 128, 0, 96), (256, 32, U, 0), (288, 32, U, 32)):
+        pick = lax.broadcasted_iota(jnp.int32, (count, 128), 0) + lane == lax.broadcasted_iota(
+            jnp.int32, (count, 128), 1
+        )
+        kinds = lax.dot_general(
+            pick.astype(F32).astype(BF16),
+            recv_ref[:, row : row + KD].reshape(K, 128),
+            (((1,), (1,)), ((), ())),
+            preferred_element_type=F32,
+        )
+        for c in range(KC):
+            part = kinds[:, c * 128 : (c + 1) * 128]
+            table[pl.ds(first * 8 + c, count, stride=8), :] = part
+            table[pl.ds(first * 8 + c + KC, count, stride=8), :] = part
     incoming[...] = jnp.zeros_like(incoming)
 
     def device(d, carry):
         def target(j, inner):
             t = d * BCAP + j
+            first = t * NI
             sums = [[jnp.zeros((8, 128), F32) for _ in range(2)] for _ in range(2)]
             for i in range(NI):
-                word = pairs[t, i]
-                n8 = pl.multiple_of(word & 0xFFFF, 8)
-                s16 = pl.multiple_of(lax.shift_right_logical(word, 16), 16)
+                n8 = pl.multiple_of(kind_rows.at[pl.ds(i, LAST)][first], 8)
+                s16 = pl.multiple_of(source_rows.at[pl.ds(i, LAST)][first], 16)
                 weight = table[pl.ds(n8, 8), :]
                 for h in range(2):
                     sums[i % 2][h] = sums[i % 2][h] + weight * ext[pl.ds(s16 + 8 * h, 8), :]
@@ -101,7 +128,7 @@
             part = incoming[pl.ds(r * KC + c, S_CL, stride=16), :].astype(BF16)
             far = far + lax.dot_general(
                 part,
-                agg[:, c * 128 : (c + 1) * 128],
+                agg[:U, c * 128 : (c + 1) * 128],
                 (((1,), (1,)), ((), ())),
                 preferred_element_type=F32,
             )
@@ -158,24 +185,18 @@
 
     send = pl.pallas_call(
         deal_kernel,
-        out_shape=jax.ShapeDtypeStruct((N_DIR, RD, BCAP, U), BF16),
-        in_specs=[VM],
-        out_specs=VM,
-        scratch_shapes=[pltpu.VMEM((R * BCAP, U), F32)],
+        out_shape=jax.ShapeDtypeStruct((N_DIR, 2 * RD * BCAP, 128), BF16),
+        in_specs=[VM, VM],
+        out_specs=VM,
+        scratch_shapes=[pltpu.VMEM((R * BCAP, 128), F32), pltpu.VMEM((KD, 384), F32)],
         name="deal",
-    )(sources)
+    )(sources, translators.T)
     recv = lax.all_to_all(send, "dir", split_axis=0, concat_axis=0, tiled=True)
-    kinds = lax.all_to_all(
-        jnp.broadcast_to(translators.T[None], (N_DIR, K // N_DIR, NTR)),
-        "dir",
-        split_axis=0,
-        concat_axis=0,
-        tiled=True,
-    ).reshape(K, NTR)
+    agg = jnp.pad(aggregate.T, ((0, 128 - U), (0, 0)))
 
     up, down = pl.pallas_call(
         boundary_kernel,
-        out_shape=[jax.ShapeDtypeStruct((RD, NBND, U), BF16)] * 2,
+        out_shape=[jax.ShapeDtypeStruct((RD, NBND, 128), BF16)] * 2,
         in_specs=[VM, VM, VM],
         out_specs=[VM, VM],
         name="boundary",
@@ -192,11 +213,10 @@
         name="near",
     )(near_columns, own_count, sources, near_blocks)
 
-    pairs = far_sources * (16 << 16) + far_translators * 8
     far = pl.pallas_call(
         far_kernel,
         out_shape=jax.ShapeDtypeStruct((N_DIR, RD, BCAP, U), BF16),
-        in_specs=[SM, SM, VM, VM, VM, VM, VM, VM],
+        in_specs=[SM, SM, SM, VM, VM, VM, VM, VM],
         out_specs=VM,
         scratch_shapes=[
             pltpu.VMEM((S_EXT * 16, 128), F32),
@@ -204,7 +224,16 @@
             pltpu.VMEM((S_CL * 16, 128), F32),
         ],
         name="far",
-    )(pairs, counts, recv, live.reshape(S_CL, 1), before, after, kinds, aggregate.T)
+    )(
+        (far_translators * 8).reshape(-1),
+        (far_sources * 16).reshape(-1),
+        counts,
+        recv,
+        live.reshape(S_CL, 1),
+        before,
+        after,
+        agg,
+    )
     back = lax.all_to_all(far, "dir", split_axis=0, concat_axis=0, tiled=True)
 
     return pl.pallas_call(

time: 134 us -> 114 us (0.85)
  blocking collectives: 33.7 us -> 0 us
  waiting for transfers between devices: 23.8 us -> 37.5 us
  Pallas kernels: 48.8 us -> 37.5 us
  starting transfers between devices: 19.5 us -> 29.2 us
    all_to_all x1 -> x0, blocking collectives: 33.7 us -> none  [per_device(): recv = lax.all_to_all(send, 'dir', split_axis=0, concat_axis=0, tiled=True)]
    all_to_all x1, waiting for transfers between devices: 10 us -> 24.5 us  [per_device(): recv = lax.all_to_all(send, 'dir', split_axis=0, concat_axis=0, tiled=True)]
    pallas_call x1, Pallas kernels: 38.2 us -> 26.5 us  [per_device(): pl.pallas_call(far_kernel, out_shape=jax.ShapeDtypeStruct((N_DIR, RD, BCA...]
    all_to_all x1, starting transfers between devices: 5.77 us -> 15.2 us  [per_device(): recv = lax.all_to_all(send, 'dir', split_axis=0, concat_axis=0, tiled=True)]
    reshape x0 -> x1, other arithmetic: none -> 1.68 us  [per_device(): (far_sources * 16).reshape(-1)]
    broadcast_in_dim x1 -> x0, local copies, waits for them, and re-layouts: 1.56 us -> none  [per_device(): jnp.broadcast_to(translators.T[None], (N_DIR, K // N_DIR, NTR))]
    unnamed x21 -> x15, local copies, waits for them, and re-layouts: 2.17 us -> 2.8 us
  transfers between devices with their start and end apart: 4 -> 4, of which waited for: 3 -> 3; matrix products, arithmetic and copies ran while one was open for 3% -> 7% of each run, Pallas kernels for 5% -> 4%
where the time goes in v2:
time: 114 us
  Pallas kernels  37.5 us (33%)
  waiting for transfers between devices  37.5 us (33%)
  starting transfers between devices  29.2 us (26%)
  local copies, waits for them, and re-layouts  6.63 us (6%)
  other arithmetic  2.93 us (3%)
    pallas_call x1, Pallas kernels, per_device(): pl.pallas_call(far_kernel, out_shape=jax.ShapeDtypeStruct((N_DIR, RD, BCA...  26.5 us
    all_to_all x1, waiting for transfers between devices, per_device(): recv = lax.all_to_all(send, 'dir', split_axis=0, concat_axis=0, tiled=True)  24.5 us
    all_to_all x1, starting transfers between devices, per_device(): recv = lax.all_to_all(send, 'dir', split_axis=0, concat_axis=0, tiled=True)  15.2 us
    all_to_all x1, waiting for transfers between devices, per_device(): back = lax.all_to_all(far, 'dir', split_axis=0, concat_axis=0, tiled=True)  12.6 us
    ppermute x2, starting transfers between devices, shifted(): lax.ppermute(value, axis, [(source, source + steps) for source in range(l...  7.66 us
    all_to_all x1, starting transfers between devices, per_device(): back = lax.all_to_all(far, 'dir', split_axis=0, concat_axis=0, tiled=True)  6.32 us
    pallas_call x1, Pallas kernels, per_device(): pl.pallas_call(near_kernel, out_shape=jax.ShapeDtypeStruct((U, BCAP * R),...  4.31 us
    unnamed x15, local copies, waits for them, and re-layouts  2.8 us
  transfers between devices with their start and end apart: 4, of which 3 were waited for; matrix products, arithmetic and copies ran while one was open for 7% of the time, Pallas kernels for 4%

profile of v2, /device:TPU:24, one launch (start us, length us, event | category | flops | bytes accessed | tf_op | source)
XLA Modules:
  0.0 113.7 jit_solution(3044733721104897745)
XLA Ops:
  0.0 0.0 copy-start.2
  0.0 2.0 %deal.1 = bf16[16,128,128]{2,1,0:T(8,128)(2,1)} custom-call(bf16[96,1024]{1,0:T(8,128)(2,1)} %src_ref.3, bf16[32,316]{1,0:T(8,128)(2,1)} %bitcast.9), custom_call_target="tpu_custom_call" | custom-call | tf_op jit(solution)/shard_map/deal/pallas_call | solution.py:186
  2.0 15.2 %all-to-all-start = ((bf16[16,128,128]{2,1,0:T(8,128)(2,1)}), bf16[16,128,128]{2,1,0:T(8,128)(2,1)S(1)}, u32[]{:S(2)}, u32[]{:S(2)}) async-start(bf16[16,128,128]{2,1,0:T(8,128)(2,1)} %deal.1), calls=%async_computation | async-start | bytes 1048576 | tf_op jit(solution)/shard_map/all_to_all | solution.py:194
  17.2 0.0 copy-start.6
  17.2 0.0 copy-start.5
  17.2 0.8 broadcast_in_dim.3
  18.0 0.1 reshape.91
  18.1 0.1 reshape.89
  18.2 1.4 %reshape.92.list_ref = s32[64,1]{1,0:T(8,128)} reshape(s32[1,2,32]{2,1,0:T(2,128)} %param.13) | data formatting | bytes 512 | tf_op jit(solution)/shard_map/reshape | solution.py:203
  19.6 0.6 compare_convert_fusion.live_ref
  20.1 1.7 %multiply_bitcast_fusion = (s32[32768]{0:T(1024)}, s32[32768]{0:T(1024)}) fusion(s32[256,128]{1,0:T(8,128)} %param.14, s32[256,128]{1,0:T(8,128)} %param.15), kind=kLoop, calls=%fused_computation | loop fusion | flops 65536 | bytes 524288 | tf_op jit(solution)/shard_map/reshape | solution.py:229
  21.8 24.5 %all-to-all-done.recv_ref = bf16[16,128,128]{2,1,0:T(8,128)(2,1)S(1)} async-done(((bf16[16,128,128]{2,1,0:T(8,128)(2,1)}), bf16[16,128,128]{2,1,0:T(8,128)(2,1)S(1)}, u32[]{:S(2)}, u32[]{:S(2)}) %all-to-all-start) | async-done | bytes 524320 | tf_op jit(solution)/shard_map/all_to_all | solution.py:194
  46.3 0.0 copy-start
  46.3 0.8 copy-done
  47.1 1.9 %boundary.1 = (bf16[4,32,128]{2,1,0:T(8,128)(2,1)}, bf16[4,32,128]{2,1,0:T(8,128)(2,1)}) custom-call(bf16[16,128,128]{2,1,0:T(8,128)(2,1)} %copy-done, s32[64,1]{1,0:T(8,128)} %reshape.92.list_ref, s32[1,256]{1,0:T(1,128)} %compare_convert_fusion.live_ref), custom_call_target="tpu_custom_call" | custom-call | tf_op jit(solution)/shard_map/boundary/pallas_call | solution.py:197
  49.0 1.9 %collective-permute-start = (bf16[4,32,128]{2,1,0:T(8,128)(2,1)}, bf16[4,32,128]{2,1,0:T(8,128)(2,1)S(1)}, u32[]{:S(2)}, u32[]{:S(2)}) collective-permute-start(bf16[4,32,128]{2,1,0:T(8,128)(2,1)} %get-tuple-element.7), channel_id=1, source_target_pairs={{0,16},{16,32},{32,48},{48,64},{64,80},{80,96},{96,112},{112,128},... | collective-permute-start | bytes 98312 | tf_op jit(solution)/shard_map/ppermute | solution.py:31
  50.9 5.8 %collective-permute-start.1 = (bf16[4,32,128]{2,1,0:T(8,128)(2,1)}, bf16[4,32,128]{2,1,0:T(8,128)(2,1)S(1)}, u32[]{:S(2)}, u32[]{:S(2)}) collective-permute-start(bf16[4,32,128]{2,1,0:T(8,128)(2,1)} %get-tuple-element.8), channel_id=1, source_target_pairs={{16,0},{32,16},{48,32},{64,48},{80,64},{96,80},{112,96},{128,112},... | collective-permute-start | bytes 98312 | tf_op jit(solution)/shard_map/ppermute | solution.py:31
  56.7 0.2 copy.15
  56.8 0.7 convert_element_type.21.live_ref
  57.5 0.0 copy-done.2
  57.5 0.7 pad.4.agg_ref
  58.2 0.0 collective-permute-done.before_ref
  58.2 0.0 copy-start.3
  58.2 0.4 collective-permute-done.1.after_ref
  58.5 0.0 copy-start.4
  58.5 0.2 copy-done.3
  58.8 0.4 copy-done.4
  59.2 26.5 %far.1 = bf16[16,4,16,96]{3,2,1,0:T(8,128)(2,1)} custom-call(s32[32768]{0:T(1024)} %get-tuple-element.10.kind_rows, s32[32768]{0:T(1024)} %get-tuple-element.9.source_rows, s32[16]{0:T(128)} %bitcast.11, bf16[16,128,128]{2,1,0:T(8,128)(2,1)} %copy-done, s32[256,1]{1,0:T(8,128)} %convert_element_type.21.live_ref, bf16[4,32,128]{2,1,0:T(8,128)(2,1)} %copy-done.3, ...), custom_call_target="tpu_custom_call" | custom-call | tf_op jit(solution)/shard_map/far/pallas_call | solution.py:216
  85.7 6.3 %all-to-all-start.1 = ((bf16[16,4,16,96]{3,2,1,0:T(8,128)(2,1)}), bf16[16,4,16,96]{3,2,1,0:T(8,128)(2,1)S(1)}, u32[]{:S(2)}, u32[]{:S(2)}) async-start(bf16[16,4,16,96]{3,2,1,0:T(8,128)(2,1)} %far.1), calls=%async_computation.1 | async-start | bytes 524288 | tf_op jit(solution)/shard_map/all_to_all | solution.py:237
  92.0 0.0 copy-done.6
  92.0 0.7 constant_dynamic-slice_fusion
  92.7 0.0 copy-done.5
  92.7 0.7 copy.17.columns
  93.4 4.3 %near.1.near_ref = f32[96,1024]{1,0:T(8,128)} custom-call(s32[16,6]{1,0:T(8,128)} %copy.17.columns, s32[1]{0:T(128)} %bitcast.count, bf16[96,1024]{1,0:T(8,128)(2,1)} %src_ref.3, bf16[16,96,576]{2,1,0:T(8,128)(2,1)} %blocks_ref.1), custom_call_target="tpu_custom_call" | custom-call | tf_op jit(solution)/shard_map/near/pallas_call | solution.py:207
  97.7 12.6 %all-to-all-done.1.back_ref = bf16[16,4,16,96]{3,2,1,0:T(8,128)(2,1)S(1)} async-done(((bf16[16,4,16,96]{3,2,1,0:T(8,128)(2,1)}), bf16[16,4,16,96]{3,2,1,0:T(8,128)(2,1)S(1)}, u32[]{:S(2)}, u32[]{:S(2)}) %all-to-all-start.1) | async-done | bytes 196640 | tf_op jit(solution)/shard_map/all_to_all | solution.py:237
  110.3 0.0 copy-start.1
  110.3 0.7 copy-done.1
  111.0 2.7 %finish.1 = bf16[96,1024]{1,0:T(8,128)(2,1)} custom-call(s32[1]{0:T(128)} %bitcast.count, bf16[16,4,16,96]{3,2,1,0:T(8,128)(2,1)} %copy-done.1, f32[96,1024]{1,0:T(8,128)} %near.1.near_ref), custom_call_target="tpu_custom_call" | custom-call | tf_op jit(solution)/shard_map/finish/pallas_call | solution.py:239
  (1 shorter events, 0.0 us)
Async XLA Ops:
  0.0 57.5 %copy-start.2 = (bf16[512,96]{0,1:T(8,128)(2,1)S(1)}, bf16[512,96]{0,1:T(8,128)(2,1)}, u32[]{:S(2)}) copy-start(bf16[512,96]{0,1:T(8,128)(2,1)} %param.11) | copy-start | bytes 294916
  2.0 44.3 %all-to-all-start = ((bf16[16,128,128]{2,1,0:T(8,128)(2,1)}), bf16[16,128,128]{2,1,0:T(8,128)(2,1)S(1)}, u32[]{:S(2)}, u32[]{:S(2)}) async-start(bf16[16,128,128]{2,1,0:T(8,128)(2,1)} %deal.1), calls=%async_computation | async-start | bytes 1048576 | tf_op jit(solution)/shard_map/all_to_all | solution.py:194
  17.2 74.8 %copy-start.6 = (s32[1,16]{1,0:T(1,128)S(1)}, s32[1,16]{1,0:T(1,128)}, u32[]{:S(2)}) copy-start(s32[1,16]{1,0:T(1,128)} %param.10) | copy-start | bytes 196
  17.2 75.5 %copy-start.5 = (s32[16,6]{0,1:T(8,128)S(1)}, s32[16,6]{0,1:T(8,128)}, u32[]{:S(2)}) copy-start(s32[16,6]{0,1:T(8,128)} %param.17) | copy-start | bytes 1156
  46.3 0.8 copy-start
  49.0 9.2 %collective-permute-start = (bf16[4,32,128]{2,1,0:T(8,128)(2,1)}, bf16[4,32,128]{2,1,0:T(8,128)(2,1)S(1)}, u32[]{:S(2)}, u32[]{:S(2)}) collective-permute-start(bf16[4,32,128]{2,1,0:T(8,128)(2,1)} %get-tuple-element.7), channel_id=1, source_target_pairs={{0,16},{16,32},{32,48},{48,64},{64,80},{80,96},{96,112},{112,128},... | collective-permute-start | bytes 98312 | tf_op jit(solution)/shard_map/ppermute | solution.py:31
  50.9 7.7 %collective-permute-start.1 = (bf16[4,32,128]{2,1,0:T(8,128)(2,1)}, bf16[4,32,128]{2,1,0:T(8,128)(2,1)S(1)}, u32[]{:S(2)}, u32[]{:S(2)}) collective-permute-start(bf16[4,32,128]{2,1,0:T(8,128)(2,1)} %get-tuple-element.8), channel_id=1, source_target_pairs={{16,0},{32,16},{48,32},{64,48},{80,64},{96,80},{112,96},{128,112},... | collective-permute-start | bytes 98312 | tf_op jit(solution)/shard_map/ppermute | solution.py:31
  58.2 0.6 copy-start.3
  58.5 0.6 copy-start.4
  85.7 24.6 %all-to-all-start.1 = ((bf16[16,4,16,96]{3,2,1,0:T(8,128)(2,1)}), bf16[16,4,16,96]{3,2,1,0:T(8,128)(2,1)S(1)}, u32[]{:S(2)}, u32[]{:S(2)}) async-start(bf16[16,4,16,96]{3,2,1,0:T(8,128)(2,1)} %far.1), calls=%async_computation.1 | async-start | bytes 524288 | tf_op jit(solution)/shard_map/all_to_all | solution.py:237
  110.3 0.7 copy-start.1

commit v3 on v2

--- a/solution.py
+++ b/solution.py
@@ -20,6 +20,7 @@
 RD = R // N_DIR
 KC = K // 128
 NTR_PAD = 320
+NHALF = NTR_PAD // 2
 LAST = (S_CL - 1) * NI + 1
 F32 = jnp.float32
 BF16 = jnp.bfloat16
@@ -39,13 +40,17 @@
             rows[pl.ds(2 * pair + half, R, stride=BCAP), :] = both[half * R : (half + 1) * R]
     wide[...] = jnp.zeros_like(wide)
     wide[:, :NTR] = kinds_ref[...].astype(F32)
-    last = wide[:, 256:384]
-    spare = jnp.concatenate([pltpu.roll(last, U, 1), pltpu.roll(last, U - KD, 1)], axis=0)
-    in_spare = lax.broadcasted_iota(jnp.int32, (RD * BCAP, 128), 1) >= U
-    tail = jnp.concatenate([wide[:, :128], wide[:, 128:256]], axis=0).astype(BF16)
+    upper = lax.axis_index("clus") % 2 == 1
+    low, mid, high = (wide[:, c * 128 : (c + 1) * 128] for c in range(3))
+    lane = lax.broadcasted_iota(jnp.int32, (KD, 128), 1)
+    shifted_up = jnp.where(lane < U, pltpu.roll(mid, U, 1), pltpu.roll(high, U, 1))
+    tail = jnp.where(upper, shifted_up, low).astype(BF16)
+    spare = jnp.where(upper, pltpu.roll(high, U - KD, 1), pltpu.roll(mid, U, 1))
     for d in range(N_DIR):
-        block = rows[d * RD * BCAP : (d + 1) * RD * BCAP, :]
-        out_ref[d, : RD * BCAP] = jnp.where(in_spare, spare, block).astype(BF16)
+        first = d * RD * BCAP
+        block = jnp.where(lane < U, rows[first : first + KD, :], spare)
+        out_ref[d, :KD] = block.astype(BF16)
+        out_ref[d, KD : RD * BCAP] = rows[first + KD : first + RD * BCAP, :].astype(BF16)
         out_ref[d, RD * BCAP :] = tail
 
 
@@ -53,7 +58,18 @@
     return recv_ref[:, r * BCAP : (r + 1) * BCAP].reshape(S_CL, 128)
 
 
-def boundary_kernel(recv_ref, list_ref, live_ref, up_ref, down_ref):
+def boundary_kernel(recv_ref, list_ref, live_ref, up_ref, down_ref, kinds_ref):
+    for first, count, lane, row in ((0, 128, 0, RD * BCAP), (128, 32, U, 0)):
+        pick = lax.broadcasted_iota(jnp.int32, (count, 128), 0) + lane == lax.broadcasted_iota(
+            jnp.int32, (count, 128), 1
+        )
+        turned = lax.dot_general(
+            pick.astype(F32).astype(BF16),
+            recv_ref[:, row : row + KD].reshape(K, 128),
+            (((1,), (1,)), ((), ())),
+            preferred_element_type=F32,
+        )
+        kinds_ref[first : first + count, :] = turned.astype(BF16)
     slots = lax.broadcasted_iota(jnp.int32, (2 * NBND, S_CL), 1)
     pick = ((slots == list_ref[...]) & (live_ref[...] > 0)).astype(F32).astype(BF16)
     for r in range(RD):
@@ -63,19 +79,35 @@
 
 
 def far_kernel(
-    kind_rows,
-    source_rows,
     counts,
+    kinds_hbm,
+    sources_hbm,
     recv_ref,
     live_ref,
     before_ref,
     after_ref,
     agg_ref,
+    mine_ref,
+    other_ref,
     out_ref,
     ext,
     table,
     incoming,
+    kind_rows,
+    source_rows,
+    sems,
 ):
+    copies = []
+    for d in range(N_DIR):
+        part = pl.ds(d * BCAP * NI, BCAP * NI)
+        copies.append(
+            (
+                pltpu.make_async_copy(kinds_hbm.at[part], kind_rows.at[part], sems.at[d, 0]),
+                pltpu.make_async_copy(sources_hbm.at[part], source_rows.at[part], sems.at[d, 1]),
+            )
+        )
+        for copy in copies[d]:
+            copy.start()
     agg = agg_ref[...]
     for r in range(RD):
         own = jnp.dot(units_of(recv_ref, r), agg, preferred_element_type=F32)
@@ -88,23 +120,20 @@
             ext[pl.ds(at, S_CL, stride=16), :] = own[:, lanes]
             ext[pl.ds(S_CL * 16 + at, NBND, stride=16), :] = prev[:, lanes]
             ext[pl.ds((S_CL + NBND) * 16 + at, NBND, stride=16), :] = foll[:, lanes]
-    for first, count, lane, row in ((0, 128, 0, 64), (128, 128, 0, 96), (256, 32, U, 0), (288, 32, U, 32)):
-        pick = lax.broadcasted_iota(jnp.int32, (count, 128), 0) + lane == lax.broadcasted_iota(
-            jnp.int32, (count, 128), 1
-        )
-        kinds = lax.dot_general(
-            pick.astype(F32).astype(BF16),
-            recv_ref[:, row : row + KD].reshape(K, 128),
-            (((1,), (1,)), ((), ())),
-            preferred_element_type=F32,
-        )
+    upper = lax.axis_index("clus") % 2 == 1
+    mine, other = mine_ref[...].astype(F32), other_ref[...].astype(F32)
+    for first, kinds in ((0, jnp.where(upper, other, mine)), (NHALF, jnp.where(upper, mine, other))):
         for c in range(KC):
             part = kinds[:, c * 128 : (c + 1) * 128]
-            table[pl.ds(first * 8 + c, count, stride=8), :] = part
-            table[pl.ds(first * 8 + c + KC, count, stride=8), :] = part
+            table[pl.ds(first * 8 + c, NHALF, stride=8), :] = part
+            table[pl.ds(first * 8 + c + KC, NHALF, stride=8), :] = part
     incoming[...] = jnp.zeros_like(incoming)
 
     def device(d, carry):
+        part = pl.ds(d * BCAP * NI, BCAP * NI)
+        pltpu.make_async_copy(kinds_hbm.at[part], kind_rows.at[part], sems.at[d, 0]).wait()
+        pltpu.make_async_copy(sources_hbm.at[part], source_rows.at[part], sems.at[d, 1]).wait()
+
         def target(j, inner):
             t = d * BCAP + j
             first = t * NI
@@ -164,6 +193,7 @@
 
 VM = pl.BlockSpec(memory_space=pltpu.VMEM)
 SM = pl.BlockSpec(memory_space=pltpu.SMEM)
+ANY = pl.BlockSpec(memory_space=pl.ANY)
 
 
 def per_device(
@@ -185,7 +215,7 @@
 
     send = pl.pallas_call(
         deal_kernel,
-        out_shape=jax.ShapeDtypeStruct((N_DIR, 2 * RD * BCAP, 128), BF16),
+        out_shape=jax.ShapeDtypeStruct((N_DIR, RD * BCAP + KD, 128), BF16),
         in_specs=[VM, VM],
         out_specs=VM,
         scratch_shapes=[pltpu.VMEM((R * BCAP, 128), F32), pltpu.VMEM((KD, 384), F32)],
@@ -194,15 +224,17 @@
     recv = lax.all_to_all(send, "dir", split_axis=0, concat_axis=0, tiled=True)
     agg = jnp.pad(aggregate.T, ((0, 128 - U), (0, 0)))
 
-    up, down = pl.pallas_call(
+    up, down, mine = pl.pallas_call(
         boundary_kernel,
-        out_shape=[jax.ShapeDtypeStruct((RD, NBND, 128), BF16)] * 2,
+        out_shape=[jax.ShapeDtypeStruct((RD, NBND, 128), BF16)] * 2
+        + [jax.ShapeDtypeStruct((NHALF, K), BF16)],
         in_specs=[VM, VM, VM],
-        out_specs=[VM, VM],
+        out_specs=[VM, VM, VM],
         name="boundary",
     )(recv, boundary_lists.reshape(2 * NBND, 1), live.reshape(1, S_CL))
     before = shifted(up, "clus", 1)
     after = shifted(down, "clus", -1)
+    other = lax.ppermute(mine, "clus", [(c, c ^ 1) for c in range(lax.axis_size("clus"))])
 
     near = pl.pallas_call(
         near_kernel,
@@ -216,23 +248,28 @@
     far = pl.pallas_call(
         far_kernel,
         out_shape=jax.ShapeDtypeStruct((N_DIR, RD, BCAP, U), BF16),
-        in_specs=[SM, SM, SM, VM, VM, VM, VM, VM],
+        in_specs=[SM, ANY, ANY, VM, VM, VM, VM, VM, VM, VM],
         out_specs=VM,
         scratch_shapes=[
             pltpu.VMEM((S_EXT * 16, 128), F32),
             pltpu.VMEM((NTR_PAD * 8, 128), F32),
             pltpu.VMEM((S_CL * 16, 128), F32),
+            pltpu.SMEM((S_CL * NI,), jnp.int32),
+            pltpu.SMEM((S_CL * NI,), jnp.int32),
+            pltpu.SemaphoreType.DMA((N_DIR, 2)),
         ],
         name="far",
     )(
+        counts,
         (far_translators * 8).reshape(-1),
         (far_sources * 16).reshape(-1),
-        counts,
         recv,
         live.reshape(S_CL, 1),
         before,
         after,
         agg,
+        mine,
+        other,
     )
     back = lax.all_to_all(far, "dir", split_axis=0, concat_axis=0, tiled=True)
 

time: 114 us -> 107 us (0.939)
  waiting for transfers between devices: 37.5 us -> 32.2 us
  Pallas kernels: 37.5 us -> 34.2 us
  starting transfers between devices: 29.2 us -> 30.8 us
    all_to_all x1, waiting for transfers between devices: 24.5 us -> 19.2 us  [per_device(): recv = lax.all_to_all(send, 'dir', split_axis=0, concat_axis=0, tiled=True)]
    pallas_call x1, Pallas kernels: 26.5 us -> 23.2 us  [per_device(): pl.pallas_call(far_kernel, out_shape=jax.ShapeDtypeStruct((N_DIR, RD, BCA...]
    ppermute x0 -> x1, starting transfers between devices: none -> 1.91 us  [per_device(): lax.ppermute(mine, 'clus', [(c, c ^ 1) for c in range(lax.axis_size('clus...]
    unnamed x15 -> x17, local copies, waits for them, and re-layouts: 2.8 us -> 2.84 us
  transfers between devices with their start and end apart: 4 -> 5, of which waited for: 3 -> 3; matrix products, arithmetic and copies ran while one was open for 7% -> 7% of each run, Pallas kernels for 4% -> 4%
where the time goes in v3:
time: 107 us
  Pallas kernels  34.2 us (32%)
  waiting for transfers between devices  32.2 us (30%)
  starting transfers between devices  30.8 us (29%)
  local copies, waits for them, and re-layouts  6.64 us (6%)
  other arithmetic  2.97 us (3%)
    pallas_call x1, Pallas kernels, per_device(): pl.pallas_call(far_kernel, out_shape=jax.ShapeDtypeStruct((N_DIR, RD, BCA...  23.2 us
    all_to_all x1, waiting for transfers between devices, per_device(): recv = lax.all_to_all(send, 'dir', split_axis=0, concat_axis=0, tiled=True)  19.2 us
    all_to_all x1, starting transfers between devices, per_device(): recv = lax.all_to_all(send, 'dir', split_axis=0, concat_axis=0, tiled=True)  15.2 us
    all_to_all x1, waiting for transfers between devices, per_device(): back = lax.all_to_all(far, 'dir', split_axis=0, concat_axis=0, tiled=True)  12.6 us
    ppermute x2, starting transfers between devices, shifted(): lax.ppermute(value, axis, [(source, source + steps) for source in range(l...  7.67 us
    all_to_all x1, starting transfers between devices, per_device(): back = lax.all_to_all(far, 'dir', split_axis=0, concat_axis=0, tiled=True)  5.99 us
    pallas_call x1, Pallas kernels, per_device(): pl.pallas_call(near_kernel, out_shape=jax.ShapeDtypeStruct((U, BCAP * R),...  4.32 us
    unnamed x17, local copies, waits for them, and re-layouts  2.84 us
  transfers between devices with their start and end apart: 5, of which 3 were waited for; matrix products, arithmetic and copies ran while one was open for 7% of the time, Pallas kernels for 4%

profile of v3, /device:TPU:24, one launch (start us, length us, event | category | flops | bytes accessed | tf_op | source)
XLA Modules:
  0.0 106.8 jit_solution(12751257070577441122)
XLA Ops:
  0.0 0.0 copy-start.3
  0.0 2.0 %deal.1 = bf16[16,96,128]{2,1,0:T(8,128)(2,1)} custom-call(bf16[96,1024]{1,0:T(8,128)(2,1)} %src_ref.3, bf16[32,316]{1,0:T(8,128)(2,1)} %bitcast.9), custom_call_target="tpu_custom_call" | custom-call | tf_op jit(solution)/shard_map/deal/pallas_call | solution.py:216
  2.0 15.2 %all-to-all-start = ((bf16[16,96,128]{2,1,0:T(8,128)(2,1)}), bf16[16,96,128]{2,1,0:T(8,128)(2,1)S(1)}, u32[]{:S(2)}, u32[]{:S(2)}) async-start(bf16[16,96,128]{2,1,0:T(8,128)(2,1)} %deal.1), calls=%async_computation | async-start | bytes 786432 | tf_op jit(solution)/shard_map/all_to_all | solution.py:224
  17.2 0.0 copy-start.7
  17.2 0.0 copy-start.6
  17.2 0.8 broadcast_in_dim.3
  18.0 0.1 reshape.91
  18.1 0.1 reshape.89
  18.1 1.4 %reshape.92.list_ref = s32[64,1]{1,0:T(8,128)} reshape(s32[1,2,32]{2,1,0:T(2,128)} %param.13) | data formatting | bytes 512 | tf_op jit(solution)/shard_map/reshape | solution.py:234
  19.5 0.6 compare_convert_fusion.live_ref
  20.1 1.7 %multiply_bitcast_fusion = (s32[32768]{0:T(1024)}, s32[32768]{0:T(1024)}) fusion(s32[256,128]{1,0:T(8,128)} %param.14, s32[256,128]{1,0:T(8,128)} %param.15), kind=kLoop, calls=%fused_computation | loop fusion | flops 65536 | bytes 524288 | tf_op jit(solution)/shard_map/reshape | solution.py:265
  21.8 19.2 %all-to-all-done.recv_ref = bf16[16,96,128]{2,1,0:T(8,128)(2,1)S(1)} async-done(((bf16[16,96,128]{2,1,0:T(8,128)(2,1)}), bf16[16,96,128]{2,1,0:T(8,128)(2,1)S(1)}, u32[]{:S(2)}, u32[]{:S(2)}) %all-to-all-start) | async-done | bytes 393248 | tf_op jit(solution)/shard_map/all_to_all | solution.py:224
  41.0 0.0 copy-start
  41.0 0.8 copy-done
  41.7 2.0 %boundary.1 = (bf16[4,32,128]{2,1,0:T(8,128)(2,1)}, bf16[4,32,128]{2,1,0:T(8,128)(2,1)}, bf16[160,512]{1,0:T(8,128)(2,1)}) custom-call(bf16[16,96,128]{2,1,0:T(8,128)(2,1)} %copy-done, s32[64,1]{1,0:T(8,128)} %reshape.92.list_ref, s32[1,256]{1,0:T(1,128)} %compare_convert_fusion.live_ref), custom_call_target="tpu_custom_call" | custom-call | tf_op jit(solution)/shard_map/boundary/pallas_call | solution.py:227
  43.7 1.9 %collective-permute-start.2 = (bf16[160,512]{1,0:T(8,128)(2,1)}, bf16[160,512]{1,0:T(8,128)(2,1)S(1)}, u32[]{:S(2)}, u32[]{:S(2)}) collective-permute-start(bf16[160,512]{1,0:T(8,128)(2,1)} %get-tuple-element.10.mine_ref), channel_id=1, source_target_pairs={{0,16},{16,0},{32,48},{48,32},{64,80},{80,64},{96,112},{112,96},{1... | collective-permute-start | bytes 491528 | tf_op jit(solution)/shard_map/ppermute | solution.py:237
  45.6 2.4 %collective-permute-start = (bf16[4,32,128]{2,1,0:T(8,128)(2,1)}, bf16[4,32,128]{2,1,0:T(8,128)(2,1)S(1)}, u32[]{:S(2)}, u32[]{:S(2)}) collective-permute-start(bf16[4,32,128]{2,1,0:T(8,128)(2,1)} %get-tuple-element.8), channel_id=1, source_target_pairs={{0,16},{16,32},{32,48},{48,64},{64,80},{80,96},{96,112},{112,128},... | collective-permute-start | bytes 98312 | tf_op jit(solution)/shard_map/ppermute | solution.py:32
  48.0 5.3 %collective-permute-start.1 = (bf16[4,32,128]{2,1,0:T(8,128)(2,1)}, bf16[4,32,128]{2,1,0:T(8,128)(2,1)S(1)}, u32[]{:S(2)}, u32[]{:S(2)}) collective-permute-start(bf16[4,32,128]{2,1,0:T(8,128)(2,1)} %get-tuple-element.9), channel_id=1, source_target_pairs={{16,0},{32,16},{48,32},{64,48},{80,64},{96,80},{112,96},{128,112},... | collective-permute-start | bytes 98312 | tf_op jit(solution)/shard_map/ppermute | solution.py:32
  53.3 0.2 copy.15
  53.5 0.7 convert_element_type.21.live_ref
  54.2 0.0 copy-done.3
  54.2 0.6 pad.4.agg_ref
  54.8 0.0 collective-permute-done.before_ref
  54.8 0.0 copy-start.4
  54.8 0.4 collective-permute-done.1.after_ref
  55.2 0.0 copy-start.5
  55.2 0.0 collective-permute-done.2.other_ref
  55.2 0.0 copy-start.2
  55.2 0.2 copy-done.4
  55.4 0.4 copy-done.5
  55.8 0.1 copy-done.2
  55.9 23.2 %far.1 = bf16[16,4,16,96]{3,2,1,0:T(8,128)(2,1)} custom-call(s32[16]{0:T(128)} %bitcast.11, s32[32768]{0:T(1024)} %get-tuple-element.12.kinds_hbm, s32[32768]{0:T(1024)} %get-tuple-element.11.sources_hbm, bf16[16,96,128]{2,1,0:T(8,128)(2,1)} %copy-done, s32[256,1]{1,0:T(8,128)} %convert_element_type.21.live_ref, bf16[4,32,128]{2,1,0:T(8,128)(2,1)} %copy-done.4, ...), custom_call_target="tpu_custom_call" | custom-call | tf_op jit(solution)/shard_map/far/pallas_call | solution.py:248
  79.1 6.0 %all-to-all-start.1 = ((bf16[16,4,16,96]{3,2,1,0:T(8,128)(2,1)}), bf16[16,4,16,96]{3,2,1,0:T(8,128)(2,1)S(1)}, u32[]{:S(2)}, u32[]{:S(2)}) async-start(bf16[16,4,16,96]{3,2,1,0:T(8,128)(2,1)} %far.1), calls=%async_computation.1 | async-start | bytes 524288 | tf_op jit(solution)/shard_map/all_to_all | solution.py:274
  85.1 0.0 copy-done.7
  85.1 0.6 constant_dynamic-slice_fusion
  85.7 0.0 copy-done.6
  85.7 0.7 copy.17.columns
  86.4 4.3 %near.1.near_ref = f32[96,1024]{1,0:T(8,128)} custom-call(s32[16,6]{1,0:T(8,128)} %copy.17.columns, s32[1]{0:T(128)} %bitcast.count, bf16[96,1024]{1,0:T(8,128)(2,1)} %src_ref.3, bf16[16,96,576]{2,1,0:T(8,128)(2,1)} %blocks_ref.1), custom_call_target="tpu_custom_call" | custom-call | tf_op jit(solution)/shard_map/near/pallas_call | solution.py:239
  90.7 12.6 %all-to-all-done.1.back_ref = bf16[16,4,16,96]{3,2,1,0:T(8,128)(2,1)S(1)} async-done(((bf16[16,4,16,96]{3,2,1,0:T(8,128)(2,1)}), bf16[16,4,16,96]{3,2,1,0:T(8,128)(2,1)S(1)}, u32[]{:S(2)}, u32[]{:S(2)}) %all-to-all-start.1) | async-done | bytes 196640 | tf_op jit(solution)/shard_map/all_to_all | solution.py:274
  103.4 0.0 copy-start.1
  103.4 0.7 copy-done.1
  104.1 2.7 %finish.1 = bf16[96,1024]{1,0:T(8,128)(2,1)} custom-call(s32[1]{0:T(128)} %bitcast.count, bf16[16,4,16,96]{3,2,1,0:T(8,128)(2,1)} %copy-done.1, f32[96,1024]{1,0:T(8,128)} %near.1.near_ref), custom_call_target="tpu_custom_call" | custom-call | tf_op jit(solution)/shard_map/finish/pallas_call | solution.py:276
  (1 shorter events, 0.0 us)
Async XLA Ops:
  0.0 54.2 %copy-start.3 = (bf16[512,96]{0,1:T(8,128)(2,1)S(1)}, bf16[512,96]{0,1:T(8,128)(2,1)}, u32[]{:S(2)}) copy-start(bf16[512,96]{0,1:T(8,128)(2,1)} %param.11) | copy-start | bytes 294916
  2.0 39.0 %all-to-all-start = ((bf16[16,96,128]{2,1,0:T(8,128)(2,1)}), bf16[16,96,128]{2,1,0:T(8,128)(2,1)S(1)}, u32[]{:S(2)}, u32[]{:S(2)}) async-start(bf16[16,96,128]{2,1,0:T(8,128)(2,1)} %deal.1), calls=%async_computation | async-start | bytes 786432 | tf_op jit(solution)/shard_map/all_to_all | solution.py:224
  17.2 67.9 %copy-start.7 = (s32[1,16]{1,0:T(1,128)S(1)}, s32[1,16]{1,0:T(1,128)}, u32[]{:S(2)}) copy-start(s32[1,16]{1,0:T(1,128)} %param.10) | copy-start | bytes 196
  17.2 68.6 %copy-start.6 = (s32[16,6]{0,1:T(8,128)S(1)}, s32[16,6]{0,1:T(8,128)}, u32[]{:S(2)}) copy-start(s32[16,6]{0,1:T(8,128)} %param.17) | copy-start | bytes 1156
  41.0 0.8 copy-start
  43.7 11.5 %collective-permute-start.2 = (bf16[160,512]{1,0:T(8,128)(2,1)}, bf16[160,512]{1,0:T(8,128)(2,1)S(1)}, u32[]{:S(2)}, u32[]{:S(2)}) collective-permute-start(bf16[160,512]{1,0:T(8,128)(2,1)} %get-tuple-element.10.mine_ref), channel_id=1, source_target_pairs={{0,16},{16,0},{32,48},{48,32},{64,80},{80,64},{96,112},{112,96},{1... | collective-permute-start | bytes 491528 | tf_op jit(solution)/shard_map/ppermute | solution.py:237
  45.6 9.2 %collective-permute-start = (bf16[4,32,128]{2,1,0:T(8,128)(2,1)}, bf16[4,32,128]{2,1,0:T(8,128)(2,1)S(1)}, u32[]{:S(2)}, u32[]{:S(2)}) collective-permute-start(bf16[4,32,128]{2,1,0:T(8,128)(2,1)} %get-tuple-element.8), channel_id=1, source_target_pairs={{0,16},{16,32},{32,48},{48,64},{64,80},{80,96},{96,112},{112,128},... | collective-permute-start | bytes 98312 | tf_op jit(solution)/shard_map/ppermute | solution.py:32
  48.0 7.2 %collective-permute-start.1 = (bf16[4,32,128]{2,1,0:T(8,128)(2,1)}, bf16[4,32,128]{2,1,0:T(8,128)(2,1)S(1)}, u32[]{:S(2)}, u32[]{:S(2)}) collective-permute-start(bf16[4,32,128]{2,1,0:T(8,128)(2,1)} %get-tuple-element.9), channel_id=1, source_target_pairs={{16,0},{32,16},{48,32},{64,48},{80,64},{96,80},{112,96},{128,112},... | collective-permute-start | bytes 98312 | tf_op jit(solution)/shard_map/ppermute | solution.py:32
  54.8 0.6 copy-start.4
  55.2 0.6 copy-start.5
  55.2 0.7 copy-start.2
  79.1 24.3 %all-to-all-start.1 = ((bf16[16,4,16,96]{3,2,1,0:T(8,128)(2,1)}), bf16[16,4,16,96]{3,2,1,0:T(8,128)(2,1)S(1)}, u32[]{:S(2)}, u32[]{:S(2)}) async-start(bf16[16,4,16,96]{3,2,1,0:T(8,128)(2,1)} %far.1), calls=%async_computation.1 | async-start | bytes 524288 | tf_op jit(solution)/shard_map/all_to_all | solution.py:274
  103.4 0.7 copy-start.1

commit v4 on v3

--- a/solution.py
+++ b/solution.py
@@ -21,15 +21,10 @@
 KC = K // 128
 NTR_PAD = 320
 NHALF = NTR_PAD // 2
+STEP = 8
 LAST = (S_CL - 1) * NI + 1
 F32 = jnp.float32
 BF16 = jnp.bfloat16
-
-
-def shifted(value, axis, steps):
-    count = lax.axis_size(axis)
-    leading, last = (max(0, -steps), min(count, count - steps))
-    return lax.ppermute(value, axis, [(source, source + steps) for source in range(leading, last)])
 
 
 def deal_kernel(src_ref, kinds_ref, out_ref, rows, wide):
@@ -58,7 +53,46 @@
     return recv_ref[:, r * BCAP : (r + 1) * BCAP].reshape(S_CL, 128)
 
 
-def boundary_kernel(recv_ref, list_ref, live_ref, up_ref, down_ref, kinds_ref):
+def pack_kernel(counts, src_ref, kind_ref, packed_kinds, packed_sources, groups_ref, spots, values, moved):
+    src, kind = src_ref[...], kind_ref[...]
+    limit = jnp.full_like(src, BCAP)
+    for d in range(N_DIR):
+        limit = jnp.where(src // BCAP == d, counts[d], limit)
+    live = src % BCAP < limit
+    flags = live.astype(F32).astype(BF16)
+    order = lax.broadcasted_iota(jnp.int32, (NI, NI), 0) <= lax.broadcasted_iota(jnp.int32, (NI, NI), 1)
+    rank = jnp.dot(flags, order.astype(F32).astype(BF16), preferred_element_type=F32)
+    spots[...] = jnp.where(live, rank - 1.0, -1.0).astype(jnp.int32)
+    total = lax.dot_general(
+        jnp.ones((8, NI), BF16), flags, (((1,), (1,)), ((), ())), preferred_element_type=F32
+    )
+    groups_ref[...] = (total.astype(jnp.int32) + STEP - 1) // STEP
+    back = S_EXT - src
+    for q, part in enumerate((back // 16 * 16, back % 16, kind // 16 * 16, kind % 16)):
+        values[pl.ds(q, S_CL, stride=8), :] = part.astype(F32)
+        values[pl.ds(q + 4, S_CL, stride=8), :] = jnp.zeros((S_CL, NI), F32)
+
+    def eight(g, carry):
+        rows = spots[pl.ds(pl.multiple_of(g * 8, 8), 8), :]
+        for j in range(8):
+            at = pl.ds(pl.multiple_of(g * 64, 64) + 8 * j, 8)
+            place = lax.broadcasted_iota(jnp.int32, (NI, NI), 0) == rows[j : j + 1, :]
+            moved[at, :] = lax.dot_general(
+                values[at, :].astype(BF16),
+                place.astype(F32).astype(BF16),
+                (((1,), (1,)), ((), ())),
+                preferred_element_type=F32,
+            )
+        return carry
+
+    lax.fori_loop(0, S_CL // 8, eight, 0)
+    parts = [moved[pl.ds(q, S_CL, stride=8), :].astype(jnp.int32) for q in range(4)]
+    packed_sources[...] = (S_EXT - parts[0] - parts[1]) * 16
+    packed_kinds[...] = (parts[2] + parts[3]) * 8
+
+
+def boundary_kernel(recv_ref, list_ref, live_ref, inner_ref, outer_ref):
+    upper = lax.axis_index("clus") % 2 == 1
     for first, count, lane, row in ((0, 128, 0, RD * BCAP), (128, 32, U, 0)):
         pick = lax.broadcasted_iota(jnp.int32, (count, 128), 0) + lane == lax.broadcasted_iota(
             jnp.int32, (count, 128), 1
@@ -68,27 +102,31 @@
             recv_ref[:, row : row + KD].reshape(K, 128),
             (((1,), (1,)), ((), ())),
             preferred_element_type=F32,
-        )
-        kinds_ref[first : first + count, :] = turned.astype(BF16)
+        ).astype(BF16)
+        for c in range(KC):
+            at = RD * NBND + c * NHALF + first
+            inner_ref[at : at + count, :] = turned[:, c * 128 : (c + 1) * 128]
     slots = lax.broadcasted_iota(jnp.int32, (2 * NBND, S_CL), 1)
     pick = ((slots == list_ref[...]) & (live_ref[...] > 0)).astype(F32).astype(BF16)
     for r in range(RD):
-        chosen = jnp.dot(pick, units_of(recv_ref, r), preferred_element_type=F32).astype(BF16)
-        up_ref[r] = chosen[:NBND]
-        down_ref[r] = chosen[NBND:]
+        chosen = jnp.dot(pick, units_of(recv_ref, r), preferred_element_type=F32)
+        up, down = chosen[:NBND], chosen[NBND:]
+        rows = slice(r * NBND, (r + 1) * NBND)
+        inner_ref[rows, :] = jnp.where(upper, down, up).astype(BF16)
+        outer_ref[rows, :] = jnp.where(upper, up, down).astype(BF16)
 
 
 def far_kernel(
     counts,
+    groups,
     kinds_hbm,
     sources_hbm,
     recv_ref,
     live_ref,
-    before_ref,
-    after_ref,
+    sent_ref,
+    inner_ref,
+    outer_ref,
     agg_ref,
-    mine_ref,
-    other_ref,
     out_ref,
     ext,
     table,
@@ -108,23 +146,26 @@
         )
         for copy in copies[d]:
             copy.start()
+    upper = lax.axis_index("clus") % 2 == 1
     agg = agg_ref[...]
     for r in range(RD):
         own = jnp.dot(units_of(recv_ref, r), agg, preferred_element_type=F32)
         own = jnp.where(live_ref[...] > 0, own, 0.0)
-        prev = jnp.dot(before_ref[r], agg, preferred_element_type=F32)
-        foll = jnp.dot(after_ref[r], agg, preferred_element_type=F32)
+        rows = slice(r * NBND, (r + 1) * NBND)
+        inner = jnp.dot(inner_ref[rows, :], agg, preferred_element_type=F32)
+        outer = jnp.dot(outer_ref[rows, :], agg, preferred_element_type=F32)
+        prev, foll = jnp.where(upper, inner, outer), jnp.where(upper, outer, inner)
         for c in range(KC):
             lanes = slice(c * 128, (c + 1) * 128)
             at = r * KC + c
             ext[pl.ds(at, S_CL, stride=16), :] = own[:, lanes]
             ext[pl.ds(S_CL * 16 + at, NBND, stride=16), :] = prev[:, lanes]
             ext[pl.ds((S_CL + NBND) * 16 + at, NBND, stride=16), :] = foll[:, lanes]
-    upper = lax.axis_index("clus") % 2 == 1
-    mine, other = mine_ref[...].astype(F32), other_ref[...].astype(F32)
-    for first, kinds in ((0, jnp.where(upper, other, mine)), (NHALF, jnp.where(upper, mine, other))):
-        for c in range(KC):
-            part = kinds[:, c * 128 : (c + 1) * 128]
+    ext[S_EXT * 16 :, :] = jnp.zeros((16, 128), F32)
+    for c in range(KC):
+        rows = slice(RD * NBND + c * NHALF, RD * NBND + (c + 1) * NHALF)
+        mine, other = sent_ref[rows, :].astype(F32), inner_ref[rows, :].astype(F32)
+        for first, part in ((0, jnp.where(upper, other, mine)), (NHALF, jnp.where(upper, mine, other))):
             table[pl.ds(first * 8 + c, NHALF, stride=8), :] = part
             table[pl.ds(first * 8 + c + KC, NHALF, stride=8), :] = part
     incoming[...] = jnp.zeros_like(incoming)
@@ -137,15 +178,28 @@
         def target(j, inner):
             t = d * BCAP + j
             first = t * NI
-            sums = [[jnp.zeros((8, 128), F32) for _ in range(2)] for _ in range(2)]
-            for i in range(NI):
-                n8 = pl.multiple_of(kind_rows.at[pl.ds(i, LAST)][first], 8)
-                s16 = pl.multiple_of(source_rows.at[pl.ds(i, LAST)][first], 16)
-                weight = table[pl.ds(n8, 8), :]
+            group = groups[0, t]
+
+            def run(count):
+                sums = [[jnp.zeros((8, 128), F32) for _ in range(2)] for _ in range(2)]
+                for i in range(count):
+                    n8 = pl.multiple_of(kind_rows.at[pl.ds(i, LAST)][first], 8)
+                    s16 = pl.multiple_of(source_rows.at[pl.ds(i, LAST)][first], 16)
+                    weight = table[pl.ds(n8, 8), :]
+                    for h in range(2):
+                        sums[i % 2][h] = sums[i % 2][h] + weight * ext[pl.ds(s16 + 8 * h, 8), :]
                 for h in range(2):
-                    sums[i % 2][h] = sums[i % 2][h] + weight * ext[pl.ds(s16 + 8 * h, 8), :]
-            for h in range(2):
-                incoming[pl.ds(pl.multiple_of(t * 16 + 8 * h, 8), 8), :] = sums[0][h] + sums[1][h]
+                    incoming[pl.ds(pl.multiple_of(t * 16 + 8 * h, 8), 8), :] = sums[0][h] + sums[1][h]
+
+            def branch(low, high):
+                if low == high:
+                    run(low * STEP)
+                    return
+                mid = (low + high) // 2
+                pl.when(group <= mid)(lambda: branch(low, mid))
+                pl.when(group > mid)(lambda: branch(mid + 1, high))
+
+            branch(0, NI // STEP)
             return inner
 
         return lax.fori_loop(0, counts[d], target, carry)
@@ -222,19 +276,23 @@
         name="deal",
     )(sources, translators.T)
     recv = lax.all_to_all(send, "dir", split_axis=0, concat_axis=0, tiled=True)
+    recv = pltpu.with_memory_space_constraint(recv, pltpu.VMEM)
     agg = jnp.pad(aggregate.T, ((0, 128 - U), (0, 0)))
 
-    up, down, mine = pl.pallas_call(
+    sent, edge = pl.pallas_call(
         boundary_kernel,
-        out_shape=[jax.ShapeDtypeStruct((RD, NBND, 128), BF16)] * 2
-        + [jax.ShapeDtypeStruct((NHALF, K), BF16)],
+        out_shape=[
+            jax.ShapeDtypeStruct((RD * NBND + KC * NHALF, 128), BF16),
+            jax.ShapeDtypeStruct((RD * NBND, 128), BF16),
+        ],
         in_specs=[VM, VM, VM],
-        out_specs=[VM, VM, VM],
+        out_specs=[VM, VM],
         name="boundary",
     )(recv, boundary_lists.reshape(2 * NBND, 1), live.reshape(1, S_CL))
-    before = shifted(up, "clus", 1)
-    after = shifted(down, "clus", -1)
-    other = lax.ppermute(mine, "clus", [(c, c ^ 1) for c in range(lax.axis_size("clus"))])
+    clusters = lax.axis_size("clus")
+    inner = lax.ppermute(sent, "clus", [(c, c ^ 1) for c in range(clusters)])
+    outer = lax.ppermute(edge, "clus", [(c, (c ^ 1) + 2 * (2 * (c % 2) - 1)) for c in range(1, clusters - 1)])
+    inner, outer = (pltpu.with_memory_space_constraint(x, pltpu.VMEM) for x in (inner, outer))
 
     near = pl.pallas_call(
         near_kernel,
@@ -245,13 +303,26 @@
         name="near",
     )(near_columns, own_count, sources, near_blocks)
 
+    kind_rows, source_rows, groups = pl.pallas_call(
+        pack_kernel,
+        out_shape=[jax.ShapeDtypeStruct((S_CL, NI), jnp.int32)] * 2
+        + [jax.ShapeDtypeStruct((8, S_CL), jnp.int32)],
+        in_specs=[SM, VM, VM],
+        out_specs=[VM, VM, VM],
+        scratch_shapes=[
+            pltpu.VMEM((S_CL, NI), jnp.int32),
+            pltpu.VMEM((S_CL * 8, NI), F32),
+            pltpu.VMEM((S_CL * 8, NI), F32),
+        ],
+        name="pack",
+    )(counts, far_sources, far_translators)
     far = pl.pallas_call(
         far_kernel,
         out_shape=jax.ShapeDtypeStruct((N_DIR, RD, BCAP, U), BF16),
-        in_specs=[SM, ANY, ANY, VM, VM, VM, VM, VM, VM, VM],
+        in_specs=[SM, SM, ANY, ANY, VM, VM, VM, VM, VM, VM],
         out_specs=VM,
         scratch_shapes=[
-            pltpu.VMEM((S_EXT * 16, 128), F32),
+            pltpu.VMEM(((S_EXT + 1) * 16, 128), F32),
             pltpu.VMEM((NTR_PAD * 8, 128), F32),
             pltpu.VMEM((S_CL * 16, 128), F32),
             pltpu.SMEM((S_CL * NI,), jnp.int32),
@@ -261,17 +332,18 @@
         name="far",
     )(
         counts,
-        (far_translators * 8).reshape(-1),
-        (far_sources * 16).reshape(-1),
+        groups,
+        kind_rows.reshape(-1),
+        source_rows.reshape(-1),
         recv,
         live.reshape(S_CL, 1),
-        before,
-        after,
+        sent,
+        inner,
+        outer,
         agg,
-        mine,
-        other,
     )
     back = lax.all_to_all(far, "dir", split_axis=0, concat_axis=0, tiled=True)
+    back = pltpu.with_memory_space_constraint(back, pltpu.VMEM)
 
     return pl.pallas_call(
         finish_kernel,

time: 107 us -> 110 us (1.028)
  Pallas kernels: 34.2 us -> 42.3 us
  starting transfers between devices: 30.8 us -> 28.2 us
  local copies, waits for them, and re-layouts: 6.64 us -> 4.46 us
  other arithmetic: 2.97 us -> 1.27 us
    pallas_call x1 -> x2, Pallas kernels: 1.95 us -> 12.3 us  [the longest x1 10.6 us: per_device(): pl.pallas_call(pack_kernel, out_shape=[jax.ShapeDtypeStruct((S_CL, NI), j...]
    ppermute x3 -> x2, starting transfers between devices: 9.58 us -> 6.86 us  [the longest x1 4.95 us: per_device(): lax.ppermute(edge, 'clus', [(c, (c ^ 1) + 2 * (2 * (c % 2) - 1)) for c in...]
    unnamed x17 -> x7, local copies, waits for them, and re-layouts: 2.84 us -> 0.69 us
    pallas_call x1, Pallas kernels: 23.2 us -> 21.2 us  [per_device(): pl.pallas_call(far_kernel, out_shape=jax.ShapeDtypeStruct((N_DIR, RD, BCA...]
    all_to_all x1, waiting for transfers between devices: 19.2 us -> 20.9 us  [per_device(): recv = lax.all_to_all(send, 'dir', split_axis=0, concat_axis=0, tiled=True)]
    reshape x1 -> x0, other arithmetic: 1.69 us -> none  [per_device(): (far_sources * 16).reshape(-1)]
  transfers between devices with their start and end apart: 5 -> 4, of which waited for: 3 -> 2; matrix products, arithmetic and copies ran while one was open for 7% -> 5% of each run, Pallas kernels for 4% -> 14%
where the time goes in v4:
time: 110 us; the launch traced here: 109 us
  Pallas kernels  42.3 us (38%)
  waiting for transfers between devices  32.8 us (30%)
  starting transfers between devices  28.2 us (26%)
  local copies, waits for them, and re-layouts  4.46 us (4%)
  other arithmetic  1.27 us (1%)
    pallas_call x1, Pallas kernels, per_device(): pl.pallas_call(far_kernel, out_shape=jax.ShapeDtypeStruct((N_DIR, RD, BCA...  21.2 us
    all_to_all x1, waiting for transfers between devices, per_device(): recv = lax.all_to_all(send, 'dir', split_axis=0, concat_axis=0, tiled=True)  20.9 us
    all_to_all x1, starting transfers between devices, per_device(): recv = lax.all_to_all(send, 'dir', split_axis=0, concat_axis=0, tiled=True)  15.3 us
    all_to_all x1, waiting for transfers between devices, per_device(): back = lax.all_to_all(far, 'dir', split_axis=0, concat_axis=0, tiled=True)  11.9 us
    pallas_call x1, Pallas kernels, per_device(): pl.pallas_call(pack_kernel, out_shape=[jax.ShapeDtypeStruct((S_CL, NI), j...  10.6 us
    all_to_all x1, starting transfers between devices, per_device(): back = lax.all_to_all(far, 'dir', split_axis=0, concat_axis=0, tiled=True)  5.99 us
    ppermute x1, starting transfers between devices, per_device(): lax.ppermute(edge, 'clus', [(c, (c ^ 1) + 2 * (2 * (c % 2) - 1)) for c in...  4.95 us
    pallas_call x1, Pallas kernels, per_device(): pl.pallas_call(near_kernel, out_shape=jax.ShapeDtypeStruct((U, BCAP * R),...  4.24 us
  transfers between devices with their start and end apart: 4, of which 2 were waited for; matrix products, arithmetic and copies ran while one was open for 5% of the time, Pallas kernels for 14%

profile of v4, /device:TPU:24, one launch (start us, length us, event | category | flops | bytes accessed | tf_op | source)
XLA Modules:
  0.0 109.0 jit_solution(17619024553596810886)
XLA Ops:
  0.0 0.0 copy-start
  0.0 2.0 %deal.1 = bf16[16,96,128]{2,1,0:T(8,128)(2,1)} custom-call(bf16[96,1024]{1,0:T(8,128)(2,1)} %src_ref.5, bf16[32,316]{1,0:T(8,128)(2,1)} %bitcast.9), custom_call_target="tpu_custom_call" | custom-call | tf_op jit(solution)/shard_map/deal/pallas_call | solution.py:270
  2.0 0.0 copy-start.1
  2.0 0.0 copy-start.2
  2.0 15.3 %all-to-all-start = ((bf16[16,96,128]{2,1,0:T(8,128)(2,1)}), bf16[16,96,128]{2,1,0:T(8,128)(2,1)S(1)}, u32[]{:S(2)}, u32[]{:S(2)}) async-start(bf16[16,96,128]{2,1,0:T(8,128)(2,1)} %deal.1), calls=%async_computation | async-start | bytes 786432 | tf_op jit(solution)/shard_map/all_to_all | solution.py:278
  17.3 0.7 broadcast_in_dim.3
  18.0 0.1 reshape.91
  18.1 0.1 reshape.89
  18.2 1.4 %reshape.92.list_ref = s32[64,1]{1,0:T(8,128)} reshape(s32[1,2,32]{2,1,0:T(2,128)} %param.13) | data formatting | bytes 512 | tf_op jit(solution)/shard_map/reshape | solution.py:291
  19.6 0.6 compare_convert_fusion.live_ref
  20.2 20.9 %all-to-all-done.recv_ref = bf16[16,96,128]{2,1,0:T(8,128)(2,1)S(1)} async-done(((bf16[16,96,128]{2,1,0:T(8,128)(2,1)}), bf16[16,96,128]{2,1,0:T(8,128)(2,1)S(1)}, u32[]{:S(2)}, u32[]{:S(2)}) %all-to-all-start) | async-done | bytes 393248 | tf_op jit(solution)/shard_map/all_to_all | solution.py:278
  41.1 1.7 %boundary.1 = (bf16[768,128]{1,0:T(8,128)(2,1)}, bf16[128,128]{1,0:T(8,128)(2,1)}) custom-call(bf16[16,96,128]{2,1,0:T(8,128)(2,1)S(1)} %all-to-all-done.recv_ref, s32[64,1]{1,0:T(8,128)} %reshape.92.list_ref, s32[1,256]{1,0:T(1,128)} %compare_convert_fusion.live_ref), custom_call_target="tpu_custom_call" | custom-call | tf_op jit(solution)/shard_map/boundary/pallas_call | solution.py:282
  42.8 1.9 %collective-permute-start = (bf16[768,128]{1,0:T(8,128)(2,1)}, bf16[768,128]{1,0:T(8,128)(2,1)S(1)}, u32[]{:S(2)}, u32[]{:S(2)}) collective-permute-start(bf16[768,128]{1,0:T(8,128)(2,1)} %get-tuple-element.13.sent_ref), channel_id=1, source_target_pairs={{0,16},{16,0},{32,48},{48,32},{64,80},{80,64},{96,112},{112,96},{1... | collective-permute-start | bytes 589832 | tf_op jit(solution)/shard_map/ppermute | solution.py:293
  44.7 4.9 %collective-permute-start.1 = (bf16[128,128]{1,0:T(8,128)(2,1)}, bf16[128,128]{1,0:T(8,128)(2,1)S(1)}, u32[]{:S(2)}, u32[]{:S(2)}) collective-permute-start(bf16[128,128]{1,0:T(8,128)(2,1)} %get-tuple-element.14), channel_id=1, source_target_pairs={{16,32},{32,16},{48,64},{64,48},{80,96},{96,80},{112,128},{128,112... | collective-permute-start | bytes 98312 | tf_op jit(solution)/shard_map/ppermute | solution.py:294
  49.7 0.2 copy.15
  49.9 0.7 convert_element_type.21.live_ref
  50.5 10.6 %pack.1 = (s32[256,128]{1,0:T(8,128)}, s32[256,128]{1,0:T(8,128)}, s32[8,256]{1,0:T(8,128)}) custom-call(s32[16]{0:T(128)} %bitcast.11, s32[256,128]{1,0:T(8,128)} %src_ref.3, s32[256,128]{1,0:T(8,128)} %kind_ref.1), custom_call_target="tpu_custom_call" | custom-call | tf_op jit(solution)/shard_map/pack/pallas_call | solution.py:306
  61.1 0.0 copy-done
  61.1 0.7 pad.4.agg_ref
  61.8 0.0 collective-permute-done.1.outer_ref
  61.8 0.0 collective-permute-done.inner_ref
  61.8 21.2 %far.1 = bf16[16,4,16,96]{3,2,1,0:T(8,128)(2,1)} custom-call(s32[16]{0:T(128)} %bitcast.12, s32[8,256]{1,0:T(8,128)} %get-tuple-element.10.groups, s32[32768]{0:T(1024)} %bitcast.6, s32[32768]{0:T(1024)} %bitcast.7, bf16[16,96,128]{2,1,0:T(8,128)(2,1)S(1)} %all-to-all-done.recv_ref, s32[256,1]{1,0:T(8,128)} %convert_element_type.21.live_ref, ...), custom_call_target="tpu_custom_call" | custom-call | tf_op jit(solution)/shard_map/far/pallas_call | solution.py:319
  83.0 6.0 %all-to-all-start.1 = ((bf16[16,4,16,96]{3,2,1,0:T(8,128)(2,1)}), bf16[16,4,16,96]{3,2,1,0:T(8,128)(2,1)S(1)}, u32[]{:S(2)}, u32[]{:S(2)}) async-start(bf16[16,4,16,96]{3,2,1,0:T(8,128)(2,1)} %far.1), calls=%async_computation.1 | async-start | bytes 524288 | tf_op jit(solution)/shard_map/all_to_all | solution.py:345
  89.0 0.0 copy-done.1
  89.0 0.6 constant_dynamic-slice_fusion
  89.7 0.0 copy-done.2
  89.7 0.7 copy.17.columns
  90.3 4.2 %near.1.near_ref = f32[96,1024]{1,0:T(8,128)} custom-call(s32[16,6]{1,0:T(8,128)} %copy.17.columns, s32[1]{0:T(128)} %bitcast.count, bf16[96,1024]{1,0:T(8,128)(2,1)} %src_ref.5, bf16[16,96,576]{2,1,0:T(8,128)(2,1)} %blocks_ref.1), custom_call_target="tpu_custom_call" | custom-call | tf_op jit(solution)/shard_map/near/pallas_call | solution.py:297
  94.6 11.9 %all-to-all-done.1.back_ref = bf16[16,4,16,96]{3,2,1,0:T(8,128)(2,1)S(1)} async-done(((bf16[16,4,16,96]{3,2,1,0:T(8,128)(2,1)}), bf16[16,4,16,96]{3,2,1,0:T(8,128)(2,1)S(1)}, u32[]{:S(2)}, u32[]{:S(2)}) %all-to-all-start.1) | async-done | bytes 196640 | tf_op jit(solution)/shard_map/all_to_all | solution.py:345
  106.5 2.6 %finish.1 = bf16[96,1024]{1,0:T(8,128)(2,1)} custom-call(s32[1]{0:T(128)} %bitcast.count, bf16[16,4,16,96]{3,2,1,0:T(8,128)(2,1)S(1)} %all-to-all-done.1.back_ref, f32[96,1024]{1,0:T(8,128)} %near.1.near_ref), custom_call_target="tpu_custom_call" | custom-call | tf_op jit(solution)/shard_map/finish/pallas_call | solution.py:348
  (1 shorter events, 0.0 us)
Async XLA Ops:
  0.0 61.1 %copy-start = (bf16[512,96]{0,1:T(8,128)(2,1)S(1)}, bf16[512,96]{0,1:T(8,128)(2,1)}, u32[]{:S(2)}) copy-start(bf16[512,96]{0,1:T(8,128)(2,1)} %param.11) | copy-start | bytes 294916
  2.0 87.0 %copy-start.1 = (s32[1,16]{1,0:T(1,128)S(1)}, s32[1,16]{1,0:T(1,128)}, u32[]{:S(2)}) copy-start(s32[1,16]{1,0:T(1,128)} %param.10) | copy-start | bytes 196
  2.0 87.7 %copy-start.2 = (s32[16,6]{0,1:T(8,128)S(1)}, s32[16,6]{0,1:T(8,128)}, u32[]{:S(2)}) copy-start(s32[16,6]{0,1:T(8,128)} %param.17) | copy-start | bytes 1156
  2.0 39.1 %all-to-all-start = ((bf16[16,96,128]{2,1,0:T(8,128)(2,1)}), bf16[16,96,128]{2,1,0:T(8,128)(2,1)S(1)}, u32[]{:S(2)}, u32[]{:S(2)}) async-start(bf16[16,96,128]{2,1,0:T(8,128)(2,1)} %deal.1), calls=%async_computation | async-start | bytes 786432 | tf_op jit(solution)/shard_map/all_to_all | solution.py:278
  42.8 19.0 %collective-permute-start = (bf16[768,128]{1,0:T(8,128)(2,1)}, bf16[768,128]{1,0:T(8,128)(2,1)S(1)}, u32[]{:S(2)}, u32[]{:S(2)}) collective-permute-start(bf16[768,128]{1,0:T(8,128)(2,1)} %get-tuple-element.13.sent_ref), channel_id=1, source_target_pairs={{0,16},{16,0},{32,48},{48,32},{64,80},{80,64},{96,112},{112,96},{1... | collective-permute-start | bytes 589832 | tf_op jit(solution)/shard_map/ppermute | solution.py:293
  44.7 17.1 %collective-permute-start.1 = (bf16[128,128]{1,0:T(8,128)(2,1)}, bf16[128,128]{1,0:T(8,128)(2,1)S(1)}, u32[]{:S(2)}, u32[]{:S(2)}) collective-permute-start(bf16[128,128]{1,0:T(8,128)(2,1)} %get-tuple-element.14), channel_id=1, source_target_pairs={{16,32},{32,16},{48,64},{64,48},{80,96},{96,80},{112,128},{128,112... | collective-permute-start | bytes 98312 | tf_op jit(solution)/shard_map/ppermute | solution.py:294
  83.0 23.5 %all-to-all-start.1 = ((bf16[16,4,16,96]{3,2,1,0:T(8,128)(2,1)}), bf16[16,4,16,96]{3,2,1,0:T(8,128)(2,1)S(1)}, u32[]{:S(2)}, u32[]{:S(2)}) async-start(bf16[16,4,16,96]{3,2,1,0:T(8,128)(2,1)} %far.1), calls=%async_computation.1 | async-start | bytes 524288 | tf_op jit(solution)/shard_map/all_to_all | solution.py:345

commit v5 on v4

--- a/solution.py
+++ b/solution.py
@@ -21,7 +21,7 @@
 KC = K // 128
 NTR_PAD = 320
 NHALF = NTR_PAD // 2
-STEP = 8
+STEP = 16
 LAST = (S_CL - 1) * NI + 1
 F32 = jnp.float32
 BF16 = jnp.bfloat16
@@ -91,7 +91,7 @@
     packed_kinds[...] = (parts[2] + parts[3]) * 8
 
 
-def boundary_kernel(recv_ref, list_ref, live_ref, inner_ref, outer_ref):
+def boundary_kernel(recv_ref, list_ref, live_ref, _, inner_ref, outer_ref):
     upper = lax.axis_index("clus") % 2 == 1
     for first, count, lane, row in ((0, 128, 0, RD * BCAP), (128, 32, U, 0)):
         pick = lax.broadcasted_iota(jnp.int32, (count, 128), 0) + lane == lax.broadcasted_iota(
@@ -196,8 +196,7 @@
                     run(low * STEP)
                     return
                 mid = (low + high) // 2
-                pl.when(group <= mid)(lambda: branch(low, mid))
-                pl.when(group > mid)(lambda: branch(mid + 1, high))
+                lax.cond(group <= mid, lambda: branch(low, mid), lambda: branch(mid + 1, high))
 
             branch(0, NI // STEP)
             return inner
@@ -205,17 +204,18 @@
         return lax.fori_loop(0, counts[d], target, carry)
 
     lax.fori_loop(0, N_DIR, device, 0)
-    for r in range(RD):
-        far = jnp.zeros((S_CL, U), F32)
-        for c in range(KC):
-            part = incoming[pl.ds(r * KC + c, S_CL, stride=16), :].astype(BF16)
-            far = far + lax.dot_general(
-                part,
-                agg[:U, c * 128 : (c + 1) * 128],
-                (((1,), (1,)), ((), ())),
-                preferred_element_type=F32,
-            )
-        out_ref[:, r] = far.reshape(N_DIR, BCAP, U).astype(BF16)
+    for r in range(RD - 1):
+        spare = jnp.concatenate([jnp.zeros((U, K), BF16), agg[r * 32 : (r + 1) * 32]], axis=0)
+        far = jnp.zeros((S_CL, 128), F32)
+        for right, side in ((r, agg), (RD - 1, spare)):
+            for c in range(KC):
+                far = far + lax.dot_general(
+                    incoming[pl.ds(right * KC + c, S_CL, stride=16), :].astype(BF16),
+                    side[:, c * 128 : (c + 1) * 128],
+                    (((1,), (1,)), ((), ())),
+                    preferred_element_type=F32,
+                )
+        out_ref[:, r * BCAP : (r + 1) * BCAP] = far.reshape(N_DIR, BCAP, 128).astype(BF16)
 
 
 def near_kernel(columns, count, src_ref, blocks_ref, out_ref, units, stack):
@@ -236,10 +236,20 @@
 
 
 def finish_kernel(count, back_ref, near_ref, out_ref, rows):
-    rows[...] = back_ref[...].astype(F32).reshape(R * BCAP, U)
+    lane = lax.broadcasted_iota(jnp.int32, (S_CL, 128), 1)
+    last = jnp.zeros((S_CL, 128), F32)
+    for r in range(RD):
+        if r < RD - 1:
+            part = back_ref[:, r * BCAP : (r + 1) * BCAP].reshape(S_CL, 128).astype(F32)
+            last = jnp.where(lane // 32 == r, pltpu.roll(part, r * 32 + 32, 1), last)
+        else:
+            part = last
+        for d in range(N_DIR):
+            first = (d * RD + r) * BCAP
+            rows[first : first + BCAP, :] = part[d * BCAP : (d + 1) * BCAP]
     for pair in range(BCAP // 2):
         halves = [rows[pl.ds(2 * pair + half, R, stride=BCAP), :] for half in range(2)]
-        far = jnp.concatenate(halves, axis=0).T
+        far = jnp.concatenate(halves, axis=0).T[:U]
         cols = slice(pair * 128, (pair + 1) * 128)
         slot = 2 * pair + lax.broadcasted_iota(jnp.int32, (U, 128), 1) // R
         out_ref[:, cols] = jnp.where(slot < count[0], far + near_ref[:, cols], 0.0).astype(BF16)
@@ -279,30 +289,6 @@
     recv = pltpu.with_memory_space_constraint(recv, pltpu.VMEM)
     agg = jnp.pad(aggregate.T, ((0, 128 - U), (0, 0)))
 
-    sent, edge = pl.pallas_call(
-        boundary_kernel,
-        out_shape=[
-            jax.ShapeDtypeStruct((RD * NBND + KC * NHALF, 128), BF16),
-            jax.ShapeDtypeStruct((RD * NBND, 128), BF16),
-        ],
-        in_specs=[VM, VM, VM],
-        out_specs=[VM, VM],
-        name="boundary",
-    )(recv, boundary_lists.reshape(2 * NBND, 1), live.reshape(1, S_CL))
-    clusters = lax.axis_size("clus")
-    inner = lax.ppermute(sent, "clus", [(c, c ^ 1) for c in range(clusters)])
-    outer = lax.ppermute(edge, "clus", [(c, (c ^ 1) + 2 * (2 * (c % 2) - 1)) for c in range(1, clusters - 1)])
-    inner, outer = (pltpu.with_memory_space_constraint(x, pltpu.VMEM) for x in (inner, outer))
-
-    near = pl.pallas_call(
-        near_kernel,
-        out_shape=jax.ShapeDtypeStruct((U, BCAP * R), F32),
-        in_specs=[SM, SM, VM, VM],
-        out_specs=VM,
-        scratch_shapes=[pltpu.VMEM((BCAP, U, R), BF16), pltpu.VMEM((NN * U, R), BF16)],
-        name="near",
-    )(near_columns, own_count, sources, near_blocks)
-
     kind_rows, source_rows, groups = pl.pallas_call(
         pack_kernel,
         out_shape=[jax.ShapeDtypeStruct((S_CL, NI), jnp.int32)] * 2
@@ -316,9 +302,33 @@
         ],
         name="pack",
     )(counts, far_sources, far_translators)
+    sent, edge = pl.pallas_call(
+        boundary_kernel,
+        out_shape=[
+            jax.ShapeDtypeStruct((RD * NBND + KC * NHALF, 128), BF16),
+            jax.ShapeDtypeStruct((RD * NBND, 128), BF16),
+        ],
+        in_specs=[VM, VM, VM, ANY],
+        out_specs=[VM, VM],
+        name="boundary",
+    )(recv, boundary_lists.reshape(2 * NBND, 1), live.reshape(1, S_CL), groups)
+    clusters = lax.axis_size("clus")
+    inner = lax.ppermute(sent, "clus", [(c, c ^ 1) for c in range(clusters)])
+    outer = lax.ppermute(edge, "clus", [(c, (c ^ 1) + 2 * (2 * (c % 2) - 1)) for c in range(1, clusters - 1)])
+    inner, outer = (pltpu.with_memory_space_constraint(x, pltpu.VMEM) for x in (inner, outer))
+
+    near = pl.pallas_call(
+        near_kernel,
+        out_shape=jax.ShapeDtypeStruct((U, BCAP * R), F32),
+        in_specs=[SM, SM, VM, VM],
+        out_specs=VM,
+        scratch_shapes=[pltpu.VMEM((BCAP, U, R), BF16), pltpu.VMEM((NN * U, R), BF16)],
+        name="near",
+    )(near_columns, own_count, sources, near_blocks)
+
     far = pl.pallas_call(
         far_kernel,
-        out_shape=jax.ShapeDtypeStruct((N_DIR, RD, BCAP, U), BF16),
+        out_shape=jax.ShapeDtypeStruct((N_DIR, (RD - 1) * BCAP, 128), BF16),
         in_specs=[SM, SM, ANY, ANY, VM, VM, VM, VM, VM, VM],
         out_specs=VM,
         scratch_shapes=[
@@ -350,7 +360,7 @@
         out_shape=jax.ShapeDtypeStruct((U, BCAP * R), BF16),
         in_specs=[SM, VM, VM],
         out_specs=VM,
-        scratch_shapes=[pltpu.VMEM((R * BCAP, U), F32)],
+        scratch_shapes=[pltpu.VMEM((R * BCAP, 128), F32)],
         name="finish",
     )(own_count, back, near)
 

time: 110 us -> 98 us (0.89)
  waiting for transfers between devices: 32.8 us -> 21.6 us
    all_to_all x1, waiting for transfers between devices: 20.9 us -> 10.3 us  [per_device(): recv = lax.all_to_all(send, 'dir', split_axis=0, concat_axis=0, tiled=True)]
    all_to_all x1, waiting for transfers between devices: 11.9 us -> 10.2 us  [per_device(): back = lax.all_to_all(far, 'dir', split_axis=0, concat_axis=0, tiled=True)]
  transfers between devices with their start and end apart: 4 -> 4, of which waited for: 2 -> 3; matrix products, arithmetic and copies ran while one was open for 5% -> 6% of each run, Pallas kernels for 14% -> 15%
where the time goes in v5:
time: 98 us; the launch traced here: 97.3 us
  Pallas kernels  41.8 us (43%)
  starting transfers between devices  28.2 us (29%)
  waiting for transfers between devices  21.6 us (22%)
  local copies, waits for them, and re-layouts  4.39 us (4%)
  other arithmetic  1.25 us (1%)
    pallas_call x1, Pallas kernels, per_device(): pl.pallas_call(far_kernel, out_shape=jax.ShapeDtypeStruct((N_DIR, (RD - 1...  20.8 us
    all_to_all x1, starting transfers between devices, per_device(): recv = lax.all_to_all(send, 'dir', split_axis=0, concat_axis=0, tiled=True)  15.3 us
    pallas_call x1, Pallas kernels, per_device(): pl.pallas_call(pack_kernel, out_shape=[jax.ShapeDtypeStruct((S_CL, NI), j...  10.6 us
    all_to_all x1, waiting for transfers between devices, per_device(): recv = lax.all_to_all(send, 'dir', split_axis=0, concat_axis=0, tiled=True)  10.3 us
    all_to_all x1, waiting for transfers between devices, per_device(): back = lax.all_to_all(far, 'dir', split_axis=0, concat_axis=0, tiled=True)  10.2 us
    all_to_all x1, starting transfers between devices, per_device(): back = lax.all_to_all(far, 'dir', split_axis=0, concat_axis=0, tiled=True)  5.99 us
    ppermute x1, starting transfers between devices, per_device(): lax.ppermute(edge, 'clus', [(c, (c ^ 1) + 2 * (2 * (c % 2) - 1)) for c in...  4.95 us
    pallas_call x1, Pallas kernels, per_device(): pl.pallas_call(near_kernel, out_shape=jax.ShapeDtypeStruct((U, BCAP * R),...  4.17 us
  transfers between devices with their start and end apart: 4, of which 3 were waited for; matrix products, arithmetic and copies ran while one was open for 6% of the time, Pallas kernels for 15%

profile of v5, /device:TPU:24, one launch (start us, length us, event | category | flops | bytes accessed | tf_op | source)
XLA Modules:
  0.0 97.3 jit_solution(8855484702345835990)
XLA Ops:
  0.0 0.0 copy-start
  0.0 2.0 %deal.1 = bf16[16,96,128]{2,1,0:T(8,128)(2,1)} custom-call(bf16[96,1024]{1,0:T(8,128)(2,1)} %src_ref.5, bf16[32,316]{1,0:T(8,128)(2,1)} %bitcast.9), custom_call_target="tpu_custom_call" | custom-call | tf_op jit(solution)/shard_map/deal/pallas_call | solution.py:280
  2.0 0.0 copy-start.1
  2.0 0.0 copy-start.2
  2.0 15.3 %all-to-all-start = ((bf16[16,96,128]{2,1,0:T(8,128)(2,1)}), bf16[16,96,128]{2,1,0:T(8,128)(2,1)S(1)}, u32[]{:S(2)}, u32[]{:S(2)}) async-start(bf16[16,96,128]{2,1,0:T(8,128)(2,1)} %deal.1), calls=%async_computation | async-start | bytes 786432 | tf_op jit(solution)/shard_map/all_to_all | solution.py:288
  17.3 0.7 broadcast_in_dim.3
  18.0 0.1 reshape.91
  18.1 0.1 reshape.89
  18.2 1.4 %reshape.92.list_ref = s32[64,1]{1,0:T(8,128)} reshape(s32[1,2,32]{2,1,0:T(2,128)} %param.13) | data formatting | bytes 512 | tf_op jit(solution)/shard_map/reshape | solution.py:314
  19.6 10.6 %pack.1 = (s32[256,128]{1,0:T(8,128)}, s32[256,128]{1,0:T(8,128)}, s32[8,256]{1,0:T(8,128)}) custom-call(s32[16]{0:T(128)} %bitcast.11, s32[256,128]{1,0:T(8,128)} %src_ref.3, s32[256,128]{1,0:T(8,128)} %kind_ref.1), custom_call_target="tpu_custom_call" | custom-call | tf_op jit(solution)/shard_map/pack/pallas_call | solution.py:292
  30.2 0.6 compare_convert_fusion.live_ref
  30.8 10.3 %all-to-all-done.recv_ref = bf16[16,96,128]{2,1,0:T(8,128)(2,1)S(1)} async-done(((bf16[16,96,128]{2,1,0:T(8,128)(2,1)}), bf16[16,96,128]{2,1,0:T(8,128)(2,1)S(1)}, u32[]{:S(2)}, u32[]{:S(2)}) %all-to-all-start) | async-done | bytes 393248 | tf_op jit(solution)/shard_map/all_to_all | solution.py:288
  41.1 1.7 %boundary.1 = (bf16[768,128]{1,0:T(8,128)(2,1)}, bf16[128,128]{1,0:T(8,128)(2,1)}) custom-call(bf16[16,96,128]{2,1,0:T(8,128)(2,1)S(1)} %all-to-all-done.recv_ref, s32[64,1]{1,0:T(8,128)} %reshape.92.list_ref, s32[1,256]{1,0:T(1,128)} %compare_convert_fusion.live_ref, s32[8,256]{1,0:T(8,128)} %get-tuple-element.10._.groups), custom_call_target="tpu_custom_call" | custom-call | tf_op jit(solution)/shard_map/boundary/pallas_call | solution.py:305
  42.8 1.9 %collective-permute-start = (bf16[768,128]{1,0:T(8,128)(2,1)}, bf16[768,128]{1,0:T(8,128)(2,1)S(1)}, u32[]{:S(2)}, u32[]{:S(2)}) collective-permute-start(bf16[768,128]{1,0:T(8,128)(2,1)} %get-tuple-element.13.sent_ref), channel_id=1, source_target_pairs={{0,16},{16,0},{32,48},{48,32},{64,80},{80,64},{96,112},{112,96},{1... | collective-permute-start | bytes 589832 | tf_op jit(solution)/shard_map/ppermute | solution.py:316
  44.7 4.9 %collective-permute-start.1 = (bf16[128,128]{1,0:T(8,128)(2,1)}, bf16[128,128]{1,0:T(8,128)(2,1)S(1)}, u32[]{:S(2)}, u32[]{:S(2)}) collective-permute-start(bf16[128,128]{1,0:T(8,128)(2,1)} %get-tuple-element.14), channel_id=1, source_target_pairs={{16,32},{32,16},{48,64},{64,48},{80,96},{96,80},{112,128},{128,112... | collective-permute-start | bytes 98312 | tf_op jit(solution)/shard_map/ppermute | solution.py:317
  49.7 0.2 copy.15
  49.8 0.7 convert_element_type.21.live_ref
  50.5 0.0 copy-done
  50.5 0.7 pad.4.agg_ref
  51.2 1.1 %collective-permute-done.1.outer_ref = bf16[128,128]{1,0:T(8,128)(2,1)S(1)} collective-permute-done((bf16[128,128]{1,0:T(8,128)(2,1)}, bf16[128,128]{1,0:T(8,128)(2,1)S(1)}, u32[]{:S(2)}, u32[]{:S(2)}) %collective-permute-start.1) | collective-permute-done | bytes 32800 | tf_op jit(solution)/shard_map/ppermute | solution.py:317
  52.3 0.0 collective-permute-done.inner_ref
  52.3 20.8 %far.1 = bf16[16,48,128]{2,1,0:T(8,128)(2,1)} custom-call(s32[16]{0:T(128)} %bitcast.12, s32[8,256]{1,0:T(8,128)} %get-tuple-element.10._.groups, s32[32768]{0:T(1024)} %bitcast.6, s32[32768]{0:T(1024)} %bitcast.7, bf16[16,96,128]{2,1,0:T(8,128)(2,1)S(1)} %all-to-all-done.recv_ref, s32[256,1]{1,0:T(8,128)} %convert_element_type.21.live_ref, ...), custom_call_target="tpu_custom_call" | custom-call | tf_op jit(solution)/shard_map/far/pallas_call | solution.py:329
  73.1 6.0 %all-to-all-start.1 = ((bf16[16,48,128]{2,1,0:T(8,128)(2,1)}), bf16[16,48,128]{2,1,0:T(8,128)(2,1)S(1)}, u32[]{:S(2)}, u32[]{:S(2)}) async-start(bf16[16,48,128]{2,1,0:T(8,128)(2,1)} %far.1), calls=%async_computation.1 | async-start | bytes 393216 | tf_op jit(solution)/shard_map/all_to_all | solution.py:355
  79.1 0.0 copy-done.1
  79.1 0.6 constant_dynamic-slice_fusion
  79.6 0.0 copy-done.2
  79.6 0.7 copy.17.columns
  80.3 4.2 %near.1.near_ref = f32[96,1024]{1,0:T(8,128)} custom-call(s32[16,6]{1,0:T(8,128)} %copy.17.columns, s32[1]{0:T(128)} %bitcast.count, bf16[96,1024]{1,0:T(8,128)(2,1)} %src_ref.5, bf16[16,96,576]{2,1,0:T(8,128)(2,1)} %blocks_ref.1), custom_call_target="tpu_custom_call" | custom-call | tf_op jit(solution)/shard_map/near/pallas_call | solution.py:320
  84.5 10.2 %all-to-all-done.1.back_ref = bf16[16,48,128]{2,1,0:T(8,128)(2,1)S(1)} async-done(((bf16[16,48,128]{2,1,0:T(8,128)(2,1)}), bf16[16,48,128]{2,1,0:T(8,128)(2,1)S(1)}, u32[]{:S(2)}, u32[]{:S(2)}) %all-to-all-start.1) | async-done | bytes 196640 | tf_op jit(solution)/shard_map/all_to_all | solution.py:355
  94.7 2.6 %finish.1 = bf16[96,1024]{1,0:T(8,128)(2,1)} custom-call(s32[1]{0:T(128)} %bitcast.count, bf16[16,48,128]{2,1,0:T(8,128)(2,1)S(1)} %all-to-all-done.1.back_ref, f32[96,1024]{1,0:T(8,128)} %near.1.near_ref), custom_call_target="tpu_custom_call" | custom-call | tf_op jit(solution)/shard_map/finish/pallas_call | solution.py:358
  (1 shorter events, 0.0 us)
Async XLA Ops:
  0.0 50.5 %copy-start = (bf16[512,96]{0,1:T(8,128)(2,1)S(1)}, bf16[512,96]{0,1:T(8,128)(2,1)}, u32[]{:S(2)}) copy-start(bf16[512,96]{0,1:T(8,128)(2,1)} %param.11) | copy-start | bytes 294916
  2.0 77.1 %copy-start.1 = (s32[1,16]{1,0:T(1,128)S(1)}, s32[1,16]{1,0:T(1,128)}, u32[]{:S(2)}) copy-start(s32[1,16]{1,0:T(1,128)} %param.10) | copy-start | bytes 196
  2.0 77.7 %copy-start.2 = (s32[16,6]{0,1:T(8,128)S(1)}, s32[16,6]{0,1:T(8,128)}, u32[]{:S(2)}) copy-start(s32[16,6]{0,1:T(8,128)} %param.17) | copy-start | bytes 1156
  2.0 39.1 %all-to-all-start = ((bf16[16,96,128]{2,1,0:T(8,128)(2,1)}), bf16[16,96,128]{2,1,0:T(8,128)(2,1)S(1)}, u32[]{:S(2)}, u32[]{:S(2)}) async-start(bf16[16,96,128]{2,1,0:T(8,128)(2,1)} %deal.1), calls=%async_computation | async-start | bytes 786432 | tf_op jit(solution)/shard_map/all_to_all | solution.py:288
  42.8 9.5 %collective-permute-start = (bf16[768,128]{1,0:T(8,128)(2,1)}, bf16[768,128]{1,0:T(8,128)(2,1)S(1)}, u32[]{:S(2)}, u32[]{:S(2)}) collective-permute-start(bf16[768,128]{1,0:T(8,128)(2,1)} %get-tuple-element.13.sent_ref), channel_id=1, source_target_pairs={{0,16},{16,0},{32,48},{48,32},{64,80},{80,64},{96,112},{112,96},{1... | collective-permute-start | bytes 589832 | tf_op jit(solution)/shard_map/ppermute | solution.py:316
  44.7 7.6 %collective-permute-start.1 = (bf16[128,128]{1,0:T(8,128)(2,1)}, bf16[128,128]{1,0:T(8,128)(2,1)S(1)}, u32[]{:S(2)}, u32[]{:S(2)}) collective-permute-start(bf16[128,128]{1,0:T(8,128)(2,1)} %get-tuple-element.14), channel_id=1, source_target_pairs={{16,32},{32,16},{48,64},{64,48},{80,96},{96,80},{112,128},{128,112... | collective-permute-start | bytes 98312 | tf_op jit(solution)/shard_map/ppermute | solution.py:317
  73.1 21.6 %all-to-all-start.1 = ((bf16[16,48,128]{2,1,0:T(8,128)(2,1)}), bf16[16,48,128]{2,1,0:T(8,128)(2,1)S(1)}, u32[]{:S(2)}, u32[]{:S(2)}) async-start(bf16[16,48,128]{2,1,0:T(8,128)(2,1)} %far.1), calls=%async_computation.1 | async-start | bytes 393216 | tf_op jit(solution)/shard_map/all_to_all | solution.py:355

commit v6 on v5

--- a/solution.py
+++ b/solution.py
@@ -21,7 +21,7 @@
 KC = K // 128
 NTR_PAD = 320
 NHALF = NTR_PAD // 2
-STEP = 16
+STEP = 8
 LAST = (S_CL - 1) * NI + 1
 F32 = jnp.float32
 BF16 = jnp.bfloat16
@@ -325,6 +325,7 @@
         scratch_shapes=[pltpu.VMEM((BCAP, U, R), BF16), pltpu.VMEM((NN * U, R), BF16)],
         name="near",
     )(near_columns, own_count, sources, near_blocks)
+    near = pltpu.with_memory_space_constraint(near, pltpu.VMEM)
 
     far = pl.pallas_call(
         far_kernel,

time: 98 us -> 98.2 us (level)
  local copies, waits for them, and re-layouts: 4.39 us -> 5.45 us
    unnamed x7 -> x9, local copies, waits for them, and re-layouts: 0.69 us -> 1.69 us
where the time goes in v6:
time: 98.2 us; the launch traced here: 97.3 us
  Pallas kernels  41.1 us (42%)
  starting transfers between devices  28.2 us (29%)
  waiting for transfers between devices  21.2 us (22%)
  local copies, waits for them, and re-layouts  5.45 us (6%)
  other arithmetic  1.24 us (1%)
    pallas_call x1, Pallas kernels, per_device(): pl.pallas_call(far_kernel, out_shape=jax.ShapeDtypeStruct((N_DIR, (RD - 1...  21 us
    all_to_all x1, starting transfers between devices, per_device(): recv = lax.all_to_all(send, 'dir', split_axis=0, concat_axis=0, tiled=True)  15.3 us
    pallas_call x1, Pallas kernels, per_device(): pl.pallas_call(pack_kernel, out_shape=[jax.ShapeDtypeStruct((S_CL, NI), j...  10.6 us
    all_to_all x1, waiting for transfers between devices, per_device(): recv = lax.all_to_all(send, 'dir', split_axis=0, concat_axis=0, tiled=True)  10.4 us
    all_to_all x1, waiting for transfers between devices, per_device(): back = lax.all_to_all(far, 'dir', split_axis=0, concat_axis=0, tiled=True)  9.78 us
    all_to_all x1, starting transfers between devices, per_device(): back = lax.all_to_all(far, 'dir', split_axis=0, concat_axis=0, tiled=True)  5.99 us
    ppermute x1, starting transfers between devices, per_device(): lax.ppermute(edge, 'clus', [(c, (c ^ 1) + 2 * (2 * (c % 2) - 1)) for c in...  4.94 us
    pallas_call x1, Pallas kernels, per_device(): pl.pallas_call(near_kernel, out_shape=jax.ShapeDtypeStruct((U, BCAP * R),...  4.26 us
  transfers between devices with their start and end apart: 4, of which 3 were waited for; matrix products, arithmetic and copies ran while one was open for 6% of the time, Pallas kernels for 15%

profile of v6, /device:TPU:24, one launch (start us, length us, event | category | flops | bytes accessed | tf_op | source)
XLA Modules:
  0.0 97.3 jit_solution(2582074002958205693)
XLA Ops:
  0.0 0.0 copy-start.1
  0.0 1.9 %deal.1 = bf16[16,96,128]{2,1,0:T(8,128)(2,1)} custom-call(bf16[96,1024]{1,0:T(8,128)(2,1)} %src_ref.5, bf16[32,316]{1,0:T(8,128)(2,1)} %bitcast.9), custom_call_target="tpu_custom_call" | custom-call | tf_op jit(solution)/shard_map/deal/pallas_call | solution.py:280
  2.0 0.0 copy-start.2
  2.0 0.0 copy-start.3
  2.0 15.3 %all-to-all-start = ((bf16[16,96,128]{2,1,0:T(8,128)(2,1)}), bf16[16,96,128]{2,1,0:T(8,128)(2,1)S(1)}, u32[]{:S(2)}, u32[]{:S(2)}) async-start(bf16[16,96,128]{2,1,0:T(8,128)(2,1)} %deal.1), calls=%async_computation | async-start | bytes 786432 | tf_op jit(solution)/shard_map/all_to_all | solution.py:288
  17.3 0.7 broadcast_in_dim.3
  18.0 0.1 reshape.91
  18.1 0.1 reshape.89
  18.2 1.4 %reshape.92.list_ref = s32[64,1]{1,0:T(8,128)} reshape(s32[1,2,32]{2,1,0:T(2,128)} %param.13) | data formatting | bytes 512 | tf_op jit(solution)/shard_map/reshape | solution.py:314
  19.6 10.6 %pack.1 = (s32[256,128]{1,0:T(8,128)}, s32[256,128]{1,0:T(8,128)}, s32[8,256]{1,0:T(8,128)}) custom-call(s32[16]{0:T(128)} %bitcast.11, s32[256,128]{1,0:T(8,128)} %src_ref.3, s32[256,128]{1,0:T(8,128)} %kind_ref.1), custom_call_target="tpu_custom_call" | custom-call | tf_op jit(solution)/shard_map/pack/pallas_call | solution.py:292
  30.2 0.6 compare_convert_fusion.live_ref
  30.7 10.4 %all-to-all-done.recv_ref = bf16[16,96,128]{2,1,0:T(8,128)(2,1)S(1)} async-done(((bf16[16,96,128]{2,1,0:T(8,128)(2,1)}), bf16[16,96,128]{2,1,0:T(8,128)(2,1)S(1)}, u32[]{:S(2)}, u32[]{:S(2)}) %all-to-all-start) | async-done | bytes 393248 | tf_op jit(solution)/shard_map/all_to_all | solution.py:288
  41.1 1.7 %boundary.1 = (bf16[768,128]{1,0:T(8,128)(2,1)}, bf16[128,128]{1,0:T(8,128)(2,1)}) custom-call(bf16[16,96,128]{2,1,0:T(8,128)(2,1)S(1)} %all-to-all-done.recv_ref, s32[64,1]{1,0:T(8,128)} %reshape.92.list_ref, s32[1,256]{1,0:T(1,128)} %compare_convert_fusion.live_ref, s32[8,256]{1,0:T(8,128)} %get-tuple-element.10._.groups), custom_call_target="tpu_custom_call" | custom-call | tf_op jit(solution)/shard_map/boundary/pallas_call | solution.py:305
  42.8 1.9 %collective-permute-start = (bf16[768,128]{1,0:T(8,128)(2,1)}, bf16[768,128]{1,0:T(8,128)(2,1)S(1)}, u32[]{:S(2)}, u32[]{:S(2)}) collective-permute-start(bf16[768,128]{1,0:T(8,128)(2,1)} %get-tuple-element.13.sent_ref), channel_id=1, source_target_pairs={{0,16},{16,0},{32,48},{48,32},{64,80},{80,64},{96,112},{112,96},{1... | collective-permute-start | bytes 589832 | tf_op jit(solution)/shard_map/ppermute | solution.py:316
  44.7 4.9 %collective-permute-start.1 = (bf16[128,128]{1,0:T(8,128)(2,1)}, bf16[128,128]{1,0:T(8,128)(2,1)S(1)}, u32[]{:S(2)}, u32[]{:S(2)}) collective-permute-start(bf16[128,128]{1,0:T(8,128)(2,1)} %get-tuple-element.14), channel_id=1, source_target_pairs={{16,32},{32,16},{48,64},{64,48},{80,96},{96,80},{112,128},{128,112... | collective-permute-start | bytes 98312 | tf_op jit(solution)/shard_map/ppermute | solution.py:317
  49.7 0.2 copy.15
  49.8 0.7 convert_element_type.21.live_ref
  50.5 0.0 copy-done.1
  50.5 0.7 pad.4.agg_ref
  51.2 1.1 %collective-permute-done.1.outer_ref = bf16[128,128]{1,0:T(8,128)(2,1)S(1)} collective-permute-done((bf16[128,128]{1,0:T(8,128)(2,1)}, bf16[128,128]{1,0:T(8,128)(2,1)S(1)}, u32[]{:S(2)}, u32[]{:S(2)}) %collective-permute-start.1) | collective-permute-done | bytes 32800 | tf_op jit(solution)/shard_map/ppermute | solution.py:317
  52.3 0.0 collective-permute-done.inner_ref
  52.3 21.0 %far.1 = bf16[16,48,128]{2,1,0:T(8,128)(2,1)} custom-call(s32[16]{0:T(128)} %bitcast.12, s32[8,256]{1,0:T(8,128)} %get-tuple-element.10._.groups, s32[32768]{0:T(1024)} %bitcast.6, s32[32768]{0:T(1024)} %bitcast.7, bf16[16,96,128]{2,1,0:T(8,128)(2,1)S(1)} %all-to-all-done.recv_ref, s32[256,1]{1,0:T(8,128)} %convert_element_type.21.live_ref, ...), custom_call_target="tpu_custom_call" | custom-call | tf_op jit(solution)/shard_map/far/pallas_call | solution.py:330
  73.2 6.0 %all-to-all-start.1 = ((bf16[16,48,128]{2,1,0:T(8,128)(2,1)}), bf16[16,48,128]{2,1,0:T(8,128)(2,1)S(1)}, u32[]{:S(2)}, u32[]{:S(2)}) async-start(bf16[16,48,128]{2,1,0:T(8,128)(2,1)} %far.1), calls=%async_computation.1 | async-start | bytes 393216 | tf_op jit(solution)/shard_map/all_to_all | solution.py:356
  79.2 0.0 copy-done.2
  79.2 0.6 constant_dynamic-slice_fusion
  79.9 0.0 copy-done.3
  79.9 0.7 copy.17.columns
  80.6 4.3 %near.1.near_ref = f32[96,1024]{1,0:T(8,128)} custom-call(s32[16,6]{1,0:T(8,128)} %copy.17.columns, s32[1]{0:T(128)} %bitcast.count, bf16[96,1024]{1,0:T(8,128)(2,1)} %src_ref.5, bf16[16,96,576]{2,1,0:T(8,128)(2,1)} %blocks_ref.1), custom_call_target="tpu_custom_call" | custom-call | tf_op jit(solution)/shard_map/near/pallas_call | solution.py:320
  84.8 9.8 %all-to-all-done.1.back_ref = bf16[16,48,128]{2,1,0:T(8,128)(2,1)S(1)} async-done(((bf16[16,48,128]{2,1,0:T(8,128)(2,1)}), bf16[16,48,128]{2,1,0:T(8,128)(2,1)S(1)}, u32[]{:S(2)}, u32[]{:S(2)}) %all-to-all-start.1) | async-done | bytes 196640 | tf_op jit(solution)/shard_map/all_to_all | solution.py:356
  94.6 0.0 copy-start
  94.6 1.0 %copy-done = f32[96,1024]{1,0:T(8,128)S(1)} copy-done((f32[96,1024]{1,0:T(8,128)S(1)}, f32[96,1024]{1,0:T(8,128)}, u32[]{:S(2)}) %copy-start) | copy-done | bytes 393240
  95.6 1.7 %finish.1 = bf16[96,1024]{1,0:T(8,128)(2,1)} custom-call(s32[1]{0:T(128)} %bitcast.count, bf16[16,48,128]{2,1,0:T(8,128)(2,1)S(1)} %all-to-all-done.1.back_ref, f32[96,1024]{1,0:T(8,128)S(1)} %copy-done), custom_call_target="tpu_custom_call" | custom-call | tf_op jit(solution)/shard_map/finish/pallas_call | solution.py:359
  (1 shorter events, 0.0 us)
Async XLA Ops:
  0.0 50.5 %copy-start.1 = (bf16[512,96]{0,1:T(8,128)(2,1)S(1)}, bf16[512,96]{0,1:T(8,128)(2,1)}, u32[]{:S(2)}) copy-start(bf16[512,96]{0,1:T(8,128)(2,1)} %param.11) | copy-start | bytes 294916
  2.0 77.3 %copy-start.2 = (s32[1,16]{1,0:T(1,128)S(1)}, s32[1,16]{1,0:T(1,128)}, u32[]{:S(2)}) copy-start(s32[1,16]{1,0:T(1,128)} %param.10) | copy-start | bytes 196
  2.0 77.9 %copy-start.3 = (s32[16,6]{0,1:T(8,128)S(1)}, s32[16,6]{0,1:T(8,128)}, u32[]{:S(2)}) copy-start(s32[16,6]{0,1:T(8,128)} %param.17) | copy-start | bytes 1156
  2.0 39.1 %all-to-all-start = ((bf16[16,96,128]{2,1,0:T(8,128)(2,1)}), bf16[16,96,128]{2,1,0:T(8,128)(2,1)S(1)}, u32[]{:S(2)}, u32[]{:S(2)}) async-start(bf16[16,96,128]{2,1,0:T(8,128)(2,1)} %deal.1), calls=%async_computation | async-start | bytes 786432 | tf_op jit(solution)/shard_map/all_to_all | solution.py:288
  42.8 9.5 %collective-permute-start = (bf16[768,128]{1,0:T(8,128)(2,1)}, bf16[768,128]{1,0:T(8,128)(2,1)S(1)}, u32[]{:S(2)}, u32[]{:S(2)}) collective-permute-start(bf16[768,128]{1,0:T(8,128)(2,1)} %get-tuple-element.13.sent_ref), channel_id=1, source_target_pairs={{0,16},{16,0},{32,48},{48,32},{64,80},{80,64},{96,112},{112,96},{1... | collective-permute-start | bytes 589832 | tf_op jit(solution)/shard_map/ppermute | solution.py:316
  44.7 7.6 %collective-permute-start.1 = (bf16[128,128]{1,0:T(8,128)(2,1)}, bf16[128,128]{1,0:T(8,128)(2,1)S(1)}, u32[]{:S(2)}, u32[]{:S(2)}) collective-permute-start(bf16[128,128]{1,0:T(8,128)(2,1)} %get-tuple-element.14), channel_id=1, source_target_pairs={{16,32},{32,16},{48,64},{64,48},{80,96},{96,80},{112,128},{128,112... | collective-permute-start | bytes 98312 | tf_op jit(solution)/shard_map/ppermute | solution.py:317
  73.2 21.4 %all-to-all-start.1 = ((bf16[16,48,128]{2,1,0:T(8,128)(2,1)}), bf16[16,48,128]{2,1,0:T(8,128)(2,1)S(1)}, u32[]{:S(2)}, u32[]{:S(2)}) async-start(bf16[16,48,128]{2,1,0:T(8,128)(2,1)} %far.1), calls=%async_computation.1 | async-start | bytes 393216 | tf_op jit(solution)/shard_map/all_to_all | solution.py:356
  94.6 1.0 %copy-start = (f32[96,1024]{1,0:T(8,128)S(1)}, f32[96,1024]{1,0:T(8,128)}, u32[]{:S(2)}) copy-start(f32[96,1024]{1,0:T(8,128)} %near.1.near_ref) | copy-start | bytes 1179652
